TPU v7x, 512 devices: a whole 4x4x16 slice. The times are simulated.
512 devices in a mesh: gx: 16 (over z), gy: 32 (over x, y, core).
Axes of the slice: x: 4, y: 4, z: 16, core: 2. Of those that a mesh axis runs over, the one named last changes fastest.
Arguments:
- labels: int32 [64, 256, 128], P('gx', 'gy'), may hold values from 0 to 16, as said below
- layer_index: int32 [128], replicated, may hold values from 0 to 7
- layer_eps: float32 [8], replicated, may hold values from 1 to 12
Outputs:
- solution_block: float32 [16, 64, 256, 128], P(None, 'gx', 'gy')
- residual_block: float32 [16, 64, 256, 128], P(None, 'gx', 'gy')
Inputs may be any that keep to these rules, and one draw needn't show every extreme that they name: `labels`: 0 marks a dielectric cell; k marks a cell of conductor k.
All inputs are finite; a program needn't handle non-finite values.
Results may differ from a plain program's by a relative error of at most 0.0003.
Values sent between devices are 32-bit elements; how exact they have to be, the bound alone decides.
No kernel may reach another device: no remote copies, remote signals or barrier semaphores. Data moves between devices by JAX's collectives and lax.ppermute only.
A program may use at most 64 MiB of HBM per device.

v0:
```python
import jax
import jax.numpy as jnp
from jax import lax
from jax.sharding import PartitionSpec as P

K = 16
ITERS = 3


def extended(block, sides, width):
    for axis, dim in sides:
        count = lax.axis_size(axis)
        forward = [(i, i + 1) for i in range(count - 1)]
        backward = [(target, source) for source, target in forward]
        low = lax.ppermute(
            lax.slice_in_dim(block, block.shape[dim] - width, None, axis=dim), axis, forward
        )
        high = lax.ppermute(lax.slice_in_dim(block, 0, width, axis=dim), axis, backward)
        block = jnp.concatenate([low, block, high], axis=dim)
    return block


def coefficients(layer_index, layer_eps):
    table = (
        layer_index[:, None] == jnp.arange(layer_eps.shape[0], dtype=jnp.int32)[None, :]
    ).astype(jnp.float32)
    eps_plane = jnp.dot(
        table, layer_eps, precision=lax.Precision.HIGHEST, preferred_element_type=jnp.float32
    )
    middle = 0.5 * (eps_plane[1:] + eps_plane[:-1])
    c_down = jnp.concatenate([eps_plane[:1], middle])
    c_up = jnp.concatenate([middle, eps_plane[-1:]])
    diagonal = 4.0 * eps_plane + c_down + c_up
    return (eps_plane, c_down, c_up, diagonal)


def laplace(padded, coeffs):
    eps_plane, c_down, c_up, diagonal = coeffs
    field = padded[:, 1:-1, 1:-1]
    lateral = (
        padded[:, 2:, 1:-1] + padded[:, :-2, 1:-1] + padded[:, 1:-1, 2:] + padded[:, 1:-1, :-2]
    )
    below = jnp.pad(field[..., :-1], ((0, 0), (0, 0), (0, 0), (1, 0)))
    above = jnp.pad(field[..., 1:], ((0, 0), (0, 0), (0, 0), (0, 1)))
    return diagonal * field - eps_plane * lateral - c_down * below - c_up * above


def local_gram(left, right):
    count = left.shape[0]
    return jnp.dot(
        left.reshape(count, -1),
        right.reshape(count, -1).T,
        precision=lax.Precision.HIGHEST,
        preferred_element_type=jnp.float32,
    )


def combine_rows(coef, field):
    count = field.shape[0]
    return jnp.dot(
        coef,
        field.reshape(count, -1),
        precision=lax.Precision.HIGHEST,
        preferred_element_type=jnp.float32,
    ).reshape(field.shape)


def lower_inverse(factor):
    count = factor.shape[0]
    inverse = jnp.zeros((count, count), jnp.float32)
    unit = jnp.eye(count, dtype=jnp.float32)
    for row in range(count):
        partial_row = unit[row] - jnp.dot(factor[row], inverse, precision=lax.Precision.HIGHEST)
        inverse = inverse.at[row].set(partial_row / factor[row, row])
    return inverse


def apply_operator(search, free, coeffs):
    padded = extended(search, (("gx", 1), ("gy", 2)), 1)
    return free * laplace(padded, coeffs)


def on_device(labels, layer_index, layer_eps):
    coeffs = coefficients(layer_index, layer_eps)
    free = (labels == 0).astype(jnp.float32)
    conductor_ids = jnp.arange(1, K + 1, dtype=jnp.int32)
    excitation = (labels[None] == conductor_ids[:, None, None, None]).astype(jnp.float32)
    padded_exc = extended(excitation, (("gx", 1), ("gy", 2)), 1)
    right_side = -free * laplace(padded_exc, coeffs)
    inverse_diag = free / coeffs[3]
    solution = jnp.zeros_like(right_side)
    residual = right_side
    prev_search = None
    prev_image = None
    for step in range(ITERS):
        precond = inverse_diag * residual
        if step == 0:
            search = precond
        else:
            beta = lax.psum(local_gram(prev_image, precond), ("gx", "gy"))
            search = precond - combine_rows(beta.T, prev_search)
        image = apply_operator(search, free, coeffs)
        curvature = lax.psum(local_gram(search, image), ("gx", "gy"))
        inverse = lower_inverse(jnp.linalg.cholesky(curvature))
        prev_search = combine_rows(inverse, search)
        prev_image = combine_rows(inverse, image)
        alpha = lax.psum(local_gram(prev_search, residual), ("gx", "gy"))
        solution = solution + combine_rows(alpha.T, prev_search)
        residual = residual - combine_rows(alpha.T, prev_image)
    return (solution, residual)


def solution(mesh):
    placed = (P("gx", "gy", None), P(), P())
    return jax.shard_map(
        on_device,
        mesh=mesh,
        in_specs=placed,
        out_specs=(P(None, "gx", "gy", None), P(None, "gx", "gy", None)),
        check_vma=False,
    )
```

profile of v0, /device:TPU:1, one launch (start us, length us, event | category | flops | bytes accessed | tf_op | source)
XLA Modules:
  0.0 967.6 jit_solution(16897844907388868109)
XLA Ops:
  1.5 4.4 collective-permute-start.1
  5.9 1.3 collective-permute-start
  8.3 1.4 add_add_fusion
  9.7 1.4 collective-permute-done
  11.1 6.7 collective-permute-start.2
  17.8 1.9 collective-permute-start.3
  19.8 1.2 collective-permute-done.3
  21.2 1.9 collective-permute-start.5
  23.1 1.3 collective-permute-start.4
  24.5 5.3 collective-permute-done.4
  29.8 2.3 collective-permute-start.6
  32.1 4.7 collective-permute-start.7
  36.9 1.0 collective-permute-done.7
  38.8 113.6 %psum.56 = f32[16,16]{0,1:T(8,128)S(1)} all-reduce(f32[16,16]{0,1:T(8,128)S(1)} %convolution_bitcast_fusion.7), channel_id=1, replica_groups=mesh['gx'=16,'gy'=32] {'gx','gy'}, use_global_device_ids=true, to_apply=%region_0.1 | all-reduce | flops 256 | bytes 2048 | tf_op jit(solution)/shard_map/psum | solution.py:103
  152.5 1.5 cholesky.59
  157.5 1.4 fusion.54
  159.0 1.5 fusion.56
  160.5 1.4 fusion.58
  161.9 1.5 fusion.60
  163.4 1.5 fusion.62
  164.9 1.5 fusion.64
  166.4 1.5 fusion.66
  167.9 1.5 fusion.68
  169.5 1.4 fusion.70
  170.9 1.5 fusion.72
  172.4 1.4 fusion.74
  173.9 1.5 fusion.76
  175.3 1.4 fusion.78
  176.8 1.5 fusion.80
  179.8 98.8 %psum.57 = f32[16,16]{1,0:T(8,128)S(1)} all-reduce(f32[16,16]{1,0:T(8,128)S(1)} %fusion.176), channel_id=1, replica_groups=mesh['gx'=16,'gy'=32] {'gx','gy'}, use_global_device_ids=true, to_apply=%region_3.5 | all-reduce | flops 256 | bytes 2048 | tf_op jit(solution)/shard_map/psum | solution.py:107
  279.7 99.6 %psum.58 = f32[16,16]{1,0:T(8,128)S(1)} all-reduce(f32[16,16]{1,0:T(8,128)S(1)} %fusion.170), channel_id=1, replica_groups=mesh['gx'=16,'gy'=32] {'gx','gy'}, use_global_device_ids=true, to_apply=%region_4.6 | all-reduce | flops 256 | bytes 2048 | tf_op jit(solution)/shard_map/psum | solution.py:100
  379.8 2.8 collective-permute-start.9
  382.6 1.3 collective-permute-start.8
  384.1 3.6 collective-permute-done.8
  387.7 4.0 collective-permute-start.10
  391.7 2.5 collective-permute-start.11
  396.2 104.3 %psum.59 = f32[16,16]{0,1:T(8,128)S(1)} all-reduce(f32[16,16]{0,1:T(8,128)S(1)} %convolution_bitcast_fusion.6), channel_id=1, replica_groups=mesh['gx'=16,'gy'=32] {'gx','gy'}, use_global_device_ids=true, to_apply=%region_5.7 | all-reduce | flops 256 | bytes 2048 | tf_op jit(solution)/shard_map/psum | solution.py:103
  500.6 1.5 cholesky.70
  505.7 1.5 fusion.86
  507.2 1.5 fusion.88
  508.6 1.4 fusion.90
  510.1 1.5 fusion.92
  511.6 1.5 fusion.94
  513.1 1.5 fusion.96
  514.6 1.5 fusion.98
  516.1 1.5 fusion.100
  517.6 1.4 fusion.102
  519.0 1.5 fusion.104
  520.6 1.4 fusion.106
  522.0 1.5 fusion.108
  523.5 1.4 fusion.110
  525.0 1.5 fusion.112
  528.1 98.5 %psum.60 = f32[16,16]{1,0:T(8,128)S(1)} all-reduce(f32[16,16]{1,0:T(8,128)S(1)} %fusion.164), channel_id=1, replica_groups=mesh['gx'=16,'gy'=32] {'gx','gy'}, use_global_device_ids=true, to_apply=%region_6.8 | all-reduce | flops 256 | bytes 2048 | tf_op jit(solution)/shard_map/psum | solution.py:107
  627.7 100.0 %psum.61 = f32[16,16]{1,0:T(8,128)S(1)} all-reduce(f32[16,16]{1,0:T(8,128)S(1)} %fusion.158), channel_id=1, replica_groups=mesh['gx'=16,'gy'=32] {'gx','gy'}, use_global_device_ids=true, to_apply=%region_7.9 | all-reduce | flops 256 | bytes 2048 | tf_op jit(solution)/shard_map/psum | solution.py:100
  728.2 2.6 collective-permute-start.13
  730.8 1.3 collective-permute-start.12
  732.6 3.3 collective-permute-done.12
  735.9 4.0 collective-permute-start.14
  739.9 2.6 collective-permute-start.15
  742.7 1.0 collective-permute-done.15
  744.6 104.5 %psum.62 = f32[16,16]{0,1:T(8,128)S(1)} all-reduce(f32[16,16]{0,1:T(8,128)S(1)} %convolution_bitcast_fusion.5), channel_id=1, replica_groups=mesh['gx'=16,'gy'=32] {'gx','gy'}, use_global_device_ids=true, to_apply=%region_8.10 | all-reduce | flops 256 | bytes 2048 | tf_op jit(solution)/shard_map/psum | solution.py:103
  849.1 1.5 cholesky.81
  859.7 0.8 fusion.132
  866.7 98.5 %psum.63 = f32[16,16]{1,0:T(8,128)S(1)} all-reduce(f32[16,16]{1,0:T(8,128)S(1)} %fusion.152), channel_id=1, replica_groups=mesh['gx'=16,'gy'=32] {'gx','gy'}, use_global_device_ids=true, to_apply=%region_9.11 | all-reduce | flops 256 | bytes 2048 | tf_op jit(solution)/shard_map/psum | solution.py:107
  (165 shorter events, 38.8 us)
Async XLA Ops:
  0.6 6.6 copy-start
  1.5 5.7 copy-start.6
  1.5 8.2 collective-permute-start.1
  5.9 5.2 collective-permute-start
  8.1 1.5 copy-start.1
  11.1 8.6 collective-permute-start.2
  17.8 3.1 collective-permute-start.3
  21.2 3.2 collective-permute-start.5
  23.1 6.6 collective-permute-start.4
  24.4 132.3 %copy-start.2 = (f32[16,16]{1,0:T(8,128)}, f32[16,16]{1,0:T(8,128)S(1)}, u32[]{:S(2)}) copy-start(f32[16,16]{1,0:T(8,128)S(1)} %fusion.220) | copy-start | bytes 3076
  29.8 7.1 collective-permute-start.6
  32.1 5.9 collective-permute-start.7
  155.3 1.4 copy-start.4
  379.8 4.3 collective-permute-start.9
  382.6 5.0 collective-permute-start.8
  387.7 6.9 collective-permute-start.10
  391.7 3.6 collective-permute-start.11
  503.4 1.4 copy-start.5
  503.4 0.7 copy-start.3
  728.2 4.3 collective-permute-start.13
  730.8 5.0 collective-permute-start.12
  735.9 6.8 collective-permute-start.14
  739.9 3.8 collective-permute-start.15
where the time goes:
time: 971 us; the launch traced here: 968 us
  blocking collectives  818 us (84%)
  matrix products  66.8 us (7%)
  starting transfers between devices  45.5 us (5%)
  waiting for transfers between devices  17.5 us (2%)
  other arithmetic  12.7 us (1%)
    psum x3, blocking collectives, on_device(): curvature = lax.psum(local_gram(search, image), ('gx', 'gy'))  322 us
    psum x3, blocking collectives, on_device(): alpha = lax.psum(local_gram(prev_search, residual), ('gx', 'gy'))  296 us
    psum x2, blocking collectives, on_device(): beta = lax.psum(local_gram(prev_image, precond), ('gx', 'gy'))  200 us
    dot_general x48, matrix products, lower_inverse(): jnp.dot(factor[row], inverse, precision=lax.Precision.HIGHEST)  55.8 us
    ppermute x8, starting transfers between devices, extended(): lax.ppermute(lax.slice_in_dim(block, block.shape[dim] - width, None, axis...  23.4 us
    ppermute x8, starting transfers between devices, extended(): lax.ppermute(lax.slice_in_dim(block, 0, width, axis=dim), axis, backward)  22.1 us
  transfers between devices with their start and end apart: 16, of which 8 were waited for; matrix products, arithmetic and copies ran while one was open for 0% of the time, Pallas kernels for 0%

commit v1 on v0

v1 whole, which is shorter than its diff:
```python
import functools

import jax
import jax.numpy as jnp
from jax import lax
from jax.experimental import pallas as pl
from jax.experimental.pallas import tpu as pltpu
from jax.sharding import PartitionSpec as P

K = 16
DEPTH = 4
HIGHEST = lax.Precision.HIGHEST


def plane_coefficients(index_ref, eps_ref):
    index = index_ref[...]
    eps = jnp.zeros(index.shape, jnp.float32)
    for layer in range(eps_ref.shape[0]):
        eps = jnp.where(index == layer, eps_ref[layer], eps)
    count = index.shape[-1]
    lane = lax.broadcasted_iota(jnp.int32, index.shape, 1)
    down = jnp.where(lane == 0, eps, 0.5 * (eps + pltpu.roll(eps, 1, 1)))
    up = jnp.where(lane == count - 1, eps, 0.5 * (eps + pltpu.roll(eps, count - 1, 1)))
    diag = 4.0 * eps + down + up
    return eps, down, up, diag, lane


def basis_kernel(place_ref, mid_ref, low_ref, high_ref, index_ref, eps_ref, basis_ref, moments_ref, lab, b0, b1, b2, b3, scaled):
    nx, wide, nz = mid_ref.shape
    ny = wide - 2 * DEPTH
    eps, down, up, diag, lane = plane_coefficients(index_ref, eps_ref)
    inverse = 1.0 / diag
    shape = (K, nz)
    lateral_c = jnp.broadcast_to(eps * inverse, shape)
    below_c = jnp.broadcast_to(jnp.where(lane == 0, 0.0, down * inverse), shape)
    above_c = jnp.broadcast_to(jnp.where(lane == nz - 1, 0.0, up * inverse), shape)
    row = lax.broadcasted_iota(jnp.int32, shape, 0) + 1
    for part, ref in enumerate((low_ref, mid_ref, high_ref)):
        inside = place_ref[part] > 0
        for x in range(nx):
            for y in range(wide):
                label = jnp.broadcast_to(ref[x, y : y + 1, :], shape)
                label = jnp.where(inside, label, -1)
                lab[part * nx + x, y] = label[:8]
                b0[part * nx + x, y] = (label == row).astype(jnp.float32)
    rows, cols = 3 * nx, wide
    bufs = (b0, b1, b2, b3, b0)
    for level in range(1, DEPTH + 1):
        source, target = bufs[level - 1], bufs[level]
        rows, cols = rows - 2, cols - 2

        def one_row(x, _, source=source, target=target, cols=cols, level=level):
            for y in range(cols):
                centre = source[x + 1, y + 1]
                lateral = (source[x, y + 1] + source[x + 2, y + 1]) + (source[x + 1, y] + source[x + 1, y + 2])
                value = (
                    lateral_c * lateral
                    + below_c * pltpu.roll(centre, 1, 1)
                    + above_c * pltpu.roll(centre, nz - 1, 1)
                )
                free = lab[x + level, y + level] == 0
                target[x, y] = jnp.where(jnp.concatenate([free, free], 0), value, 0.0)
            return 0

        lax.fori_loop(0, rows, one_row, 0)
    for power in range(4):
        inset = DEPTH - 1 - power
        for x in range(nx):
            for y in range(ny):
                value = bufs[power + 1][x + inset, y + inset]
                cell = x * ny + y
                basis_ref[power * K : (power + 1) * K, cell * nz : (cell + 1) * nz] = value
                scaled[power * K : (power + 1) * K, cell * nz : (cell + 1) * nz] = value * diag
    gram = lax.dot_general(
        basis_ref[: 3 * K, :],
        scaled[...],
        (((1,), (1,)), ((), ())),
        precision=HIGHEST,
        preferred_element_type=jnp.float32,
    )
    gram = jnp.concatenate([gram, jnp.zeros((3 * K, 128 - 4 * K), jnp.float32)], 1)
    place = lax.broadcasted_iota(jnp.int32, (K, 128), 1)
    moments = jnp.where(
        place < 2 * K,
        gram[:K],
        jnp.where(
            place < 4 * K,
            pltpu.roll(gram[K : 2 * K], K, 1),
            jnp.where(place < 6 * K, pltpu.roll(gram[2 * K :], 2 * K, 1), 0.0),
        ),
    )
    for copy in range(moments_ref.shape[0]):
        moments_ref[copy] = moments


def outputs_kernel(parts_ref, basis_ref, index_ref, eps_ref, solution_ref, residual_ref):
    ny, nz = solution_ref.shape[2:]
    cells = solution_ref.shape[1] * ny
    _, _, _, diag, _ = plane_coefficients(index_ref, eps_ref)
    moments = parts_ref[0]
    for part in range(1, parts_ref.shape[0]):
        moments = moments + parts_ref[part]
    place = lax.broadcasted_iota(jnp.int32, (K, 128), 1)
    images = moments - pltpu.roll(moments, 128 - K, 1)
    blocks = []
    for power in range(3):
        left = images if power == 0 else pltpu.roll(images, 128 - power * K, 1)
        right = moments if power == 3 else pltpu.roll(moments, (3 - power) * K, 1)
        blocks.append(jnp.where(place < 3 * K, left, jnp.where(place < 4 * K, right, 0.0)))
    matrix = jnp.concatenate(blocks, 0)
    number = lax.broadcasted_iota(jnp.int32, (3 * K, 128), 0)
    for pivot in range(3 * K):
        line = matrix[pivot : pivot + 1, :]
        line = line * (1.0 / matrix[pivot : pivot + 1, pivot : pivot + 1])
        column = jnp.broadcast_to(matrix[:, pivot : pivot + 1], matrix.shape)
        matrix = jnp.where(number == pivot, line, matrix - column * line)
    weights = matrix[:, 3 * K : 4 * K].T
    first, second, third = weights[:, :K], weights[:, K : 2 * K], weights[:, 2 * K :]
    unit = (
        lax.broadcasted_iota(jnp.int32, (K, K), 0) == lax.broadcasted_iota(jnp.int32, (K, K), 1)
    ).astype(jnp.float32)
    combine = jnp.concatenate(
        [
            jnp.concatenate([first, second, third, jnp.zeros((K, K), jnp.float32)], 1),
            jnp.concatenate([unit - first, first - second, second - third, third], 1),
        ],
        0,
    )
    both = jnp.dot(combine, basis_ref[...], precision=HIGHEST, preferred_element_type=jnp.float32)
    for cell in range(cells):
        block = both[:, cell * nz : (cell + 1) * nz]
        solution_ref[:, cell // ny, cell % ny, :] = block[:K]
        residual_ref[:, cell // ny, cell % ny, :] = block[K:] * diag


def neighbours(block, axis):
    count = lax.axis_size(axis)
    forward = [(i, i + 1) for i in range(count - 1)]
    backward = [(target, source) for source, target in forward]
    return lax.ppermute(block, axis, forward), lax.ppermute(block, axis, backward)


def gathered(copies, axis):
    return lax.all_to_all(copies, axis, 0, 0, tiled=True)


def on_device(labels, layer_index, layer_eps):
    nx, ny, nz = labels.shape
    wide = ny + 2 * DEPTH
    in_x, in_y = lax.axis_size("gx"), lax.axis_size("gy")
    at_x, at_y = lax.axis_index("gx"), lax.axis_index("gy")
    before, after = neighbours(labels, "gy")
    mid = jnp.concatenate(
        [
            jnp.where(at_y > 0, before[:, ny - DEPTH :], -1),
            labels,
            jnp.where(at_y < in_y - 1, after[:, :DEPTH], -1),
        ],
        1,
    )
    low, high = neighbours(mid, "gx")
    place = jnp.stack([at_x > 0, at_x >= 0, at_x < in_x - 1]).astype(jnp.int32)
    index = layer_index.reshape(1, nz)
    vmem, smem = pl.BlockSpec(memory_space=pltpu.VMEM), pl.BlockSpec(memory_space=pltpu.SMEM)
    rows = 3 * nx
    basis, moments = pl.pallas_call(
        basis_kernel,
        out_shape=(
            jax.ShapeDtypeStruct((4 * K, nx * ny * nz), jnp.float32),
            jax.ShapeDtypeStruct((in_y, K, 128), jnp.float32),
        ),
        in_specs=[smem, vmem, vmem, vmem, vmem, smem],
        out_specs=(vmem, vmem),
        scratch_shapes=[pltpu.VMEM((rows, wide, 8, nz), jnp.int32)]
        + [pltpu.VMEM((rows - 2 * i, wide - 2 * i, K, nz), jnp.float32) for i in range(4)]
        + [pltpu.VMEM((4 * K, nx * ny * nz), jnp.float32)],
        compiler_params=pltpu.CompilerParams(vmem_limit_bytes=16 << 20),
    )(place, mid, low, high, index, layer_eps)
    total = gathered(moments, "gy").sum(0)
    parts = gathered(jnp.broadcast_to(total[None], (in_x,) + total.shape), "gx")
    block = jax.ShapeDtypeStruct((K, nx, ny, nz), jnp.float32)
    return pl.pallas_call(
        outputs_kernel,
        out_shape=(block, block),
        in_specs=[vmem, vmem, vmem, smem],
        out_specs=(vmem, vmem),
        compiler_params=pltpu.CompilerParams(vmem_limit_bytes=16 << 20),
    )(parts, basis, index, layer_eps)


def solution(mesh):
    return jax.shard_map(
        on_device,
        mesh=mesh,
        in_specs=(P("gx", "gy", None), P(), P()),
        out_specs=(P(None, "gx", "gy", None), P(None, "gx", "gy", None)),
        check_vma=False,
    )
```

time: 971 us -> 75 us (0.08)
  blocking collectives: 818 us -> 44.3 us
  matrix products: 66.8 us -> 0 us
  starting transfers between devices: 45.5 us -> 15.4 us
  waiting for transfers between devices: 17.5 us -> 1.9 us
  other arithmetic: 12.7 us -> 0.14 us
  Pallas kernels: 0 us -> 11.6 us
    psum x8 -> x0, blocking collectives: 818 us -> none  [the longest x3 322 us: on_device(): curvature = lax.psum(local_gram(search, image), ('gx', 'gy'))]
    dot_general x71 -> x0, matrix products: 66.8 us -> none  [the longest x48 55.8 us: lower_inverse(): jnp.dot(factor[row], inverse, precision=lax.Precision.HIGHEST)]
    all_to_all x0 -> x2, blocking collectives: none -> 44.3 us  [gathered(): return lax.all_to_all(copies, axis, 0, 0, tiled=True)]
    ppermute x16 -> x4, starting transfers between devices: 45.5 us -> 15.4 us  [the longest x2 8.58 us: neighbours(): lax.ppermute(block, axis, forward)]
    ppermute x16 -> x4, waiting for transfers between devices: 17.5 us -> 1.9 us  [the longest x2 0.98 us: neighbours(): lax.ppermute(block, axis, backward)]
    pallas_call x0 -> x2, Pallas kernels: none -> 11.6 us  [the longest x1 6.49 us: on_device(): pl.pallas_call(outputs_kernel, out_shape=(block, block), in_specs=[vmem,...]
  transfers between devices with their start and end apart: 16 -> 4, of which waited for: 8 -> 2; matrix products, arithmetic and copies ran while one was open for 0% -> 0% of each run, Pallas kernels for 0% -> 0%
where the time goes in v1:
time: 75 us; the launch traced here: 74 us
  blocking collectives  44.3 us (59%)
  starting transfers between devices  15.4 us (21%)
  Pallas kernels  11.6 us (15%)
  waiting for transfers between devices  1.9 us (3%)
    all_to_all x2, blocking collectives, gathered(): return lax.all_to_all(copies, axis, 0, 0, tiled=True)  44.3 us
    ppermute x2, starting transfers between devices, neighbours(): lax.ppermute(block, axis, forward)  8.58 us
    ppermute x2, starting transfers between devices, neighbours(): lax.ppermute(block, axis, backward)  6.77 us
    pallas_call x1, Pallas kernels, on_device(): pl.pallas_call(outputs_kernel, out_shape=(block, block), in_specs=[vmem,...  6.49 us
    pallas_call x1, Pallas kernels, on_device(): pl.pallas_call(basis_kernel, out_shape=(jax.ShapeDtypeStruct((4 * K, nx *...  5.08 us
  transfers between devices with their start and end apart: 4, of which 2 were waited for; matrix products, arithmetic and copies ran while one was open for 0% of the time, Pallas kernels for 0%

profile of v1, /device:TPU:1, one launch (start us, length us, event | category | flops | bytes accessed | tf_op | source)
XLA Modules:
  0.0 74.0 jit_solution(16791799449290467822)
XLA Ops:
  0.6 4.6 %collective-permute-start = (s32[4,8,128]{2,1,0:T(8,128)}, s32[4,8,128]{2,1,0:T(8,128)S(1)}, u32[]{:S(2)}, u32[]{:S(2)}) collective-permute-start(s32[4,8,128]{2,1,0:T(8,128)} %param.3), channel_id=1, source_target_pairs={{0,1},{1,2},{2,3},{3,4},{4,5},{5,6},{6,7},{7,8},{8,9},{9,10},{10,1... | collective-permute-start | bytes 49160 | tf_op jit(solution)/shard_map/ppermute | solution.py:140
  5.2 5.5 %collective-permute-start.1 = (s32[4,8,128]{2,1,0:T(8,128)}, s32[4,8,128]{2,1,0:T(8,128)S(1)}, u32[]{:S(2)}, u32[]{:S(2)}) collective-permute-start(s32[4,8,128]{2,1,0:T(8,128)} %param.3), channel_id=1, source_target_pairs={{1,0},{2,1},{3,2},{4,3},{5,4},{6,5},{7,6},{8,7},{9,8},{10,9},{11,1... | collective-permute-start | bytes 49160 | tf_op jit(solution)/shard_map/ppermute | solution.py:140
  10.7 0.0 copy-start.2
  10.7 0.0 collective-permute-done
  10.8 1.0 %collective-permute-done.1 = s32[4,8,128]{2,1,0:T(8,128)S(1)} collective-permute-done((s32[4,8,128]{2,1,0:T(8,128)}, s32[4,8,128]{2,1,0:T(8,128)S(1)}, u32[]{:S(2)}, u32[]{:S(2)}) %collective-permute-start.1) | collective-permute-done | bytes 16416 | tf_op jit(solution)/shard_map/ppermute | solution.py:140
  11.8 0.0 copy-done.2
  11.8 1.3 %collective-permute-start.3 = (s32[4,16,128]{2,1,0:T(8,128)S(1)}, s32[4,16,128]{2,1,0:T(8,128)S(1)}, u32[]{:S(2)}, u32[]{:S(2)}) collective-permute-start(s32[4,16,128]{2,1,0:T(8,128)S(1)} %pad_add_fusion.mid_ref), channel_id=1, source_target_pairs={{32,0},{64,32},{96,64},{128,96},{160,128},{192,160},{224,192},{256... | collective-permute-start | bytes 98312 | tf_op jit(solution)/shard_map/ppermute | solution.py:140
  13.1 4.0 %collective-permute-start.2 = (s32[4,16,128]{2,1,0:T(8,128)S(1)}, s32[4,16,128]{2,1,0:T(8,128)S(1)}, u32[]{:S(2)}, u32[]{:S(2)}) collective-permute-start(s32[4,16,128]{2,1,0:T(8,128)S(1)} %pad_add_fusion.mid_ref), channel_id=1, source_target_pairs={{0,32},{32,64},{64,96},{96,128},{128,160},{160,192},{192,224},{224... | collective-permute-start | bytes 98312 | tf_op jit(solution)/shard_map/ppermute | solution.py:140
  17.1 0.1 add_convert_fusion.place_ref
  17.1 0.0 copy-start
  17.1 0.0 copy-start.1
  17.2 0.0 collective-permute-done.3.high_ref
  17.2 0.9 %collective-permute-done.2.low_ref = s32[4,16,128]{2,1,0:T(8,128)S(1)} collective-permute-done((s32[4,16,128]{2,1,0:T(8,128)S(1)}, s32[4,16,128]{2,1,0:T(8,128)S(1)}, u32[]{:S(2)}, u32[]{:S(2)}) %collective-permute-start.2) | collective-permute-done | bytes 32800 | tf_op jit(solution)/shard_map/ppermute | solution.py:140
  18.1 0.0 copy-done
  18.1 0.0 copy-done.1
  18.1 5.1 %shard_map.50 = (f32[64,4096]{1,0:T(8,128)S(1)}, f32[32,16,128]{2,1,0:T(8,128)S(1)}) custom-call(s32[3]{0:T(128)S(1)} %add_convert_fusion.place_ref, s32[4,16,128]{2,1,0:T(8,128)S(1)} %pad_add_fusion.mid_ref, s32[4,16,128]{2,1,0:T(8,128)S(1)} %collective-permute-done.2.low_ref, s32[4,16,128]{2,1,0:T(8,128)S(1)} %collective-permute-done.3.high_ref, ...), custom_call_target="tpu_custom_call" | custom-call | tf_op jit(solution)/shard_map/pallas_call | solution.py:166
  23.2 16.1 %all_to_all.10 = f32[32,16,128]{2,1,0:T(8,128)S(1)} all-to-all(f32[32,16,128]{2,1,0:T(8,128)S(1)} %get-tuple-element.4), channel_id=1, replica_groups=mesh['gx'=16,'gy'=32] {'gy'}, dimensions={0} | all-to-all | bytes 524288 | tf_op jit(solution)/shard_map/all_to_all | solution.py:144
  39.4 28.2 %all_to_all.11.parts_ref = f32[16,16,128]{2,1,0:T(8,128)S(1)} all-to-all(f32[16,16,128]{2,1,0:T(8,128)S(1)} %broadcast_in_dim.12), channel_id=1, replica_groups=mesh['gx'=16,'gy'=32] {'gx'}, dimensions={0} | all-to-all | bytes 262144 | tf_op jit(solution)/shard_map/all_to_all | solution.py:144
  67.5 6.5 %shard_map.51 = (f32[16,4,8,128]{3,2,1,0:T(8,128)}, f32[16,4,8,128]{3,2,1,0:T(8,128)}) custom-call(f32[16,16,128]{2,1,0:T(8,128)S(1)} %all_to_all.11.parts_ref, f32[64,4096]{1,0:T(8,128)S(1)} %get-tuple-element.5.basis_ref, s32[1,128]{1,0:T(1,128)S(1)} %bitcast.5, f32[8]{0:T(128)S(1)} %copy-done.1), custom_call_target="tpu_custom_call" | custom-call | tf_op jit(solution)/shard_map/pallas_call | solution.py:182
  (5 shorter events, 0.1 us)
Async XLA Ops:
  0.6 10.1 %collective-permute-start = (s32[4,8,128]{2,1,0:T(8,128)}, s32[4,8,128]{2,1,0:T(8,128)S(1)}, u32[]{:S(2)}, u32[]{:S(2)}) collective-permute-start(s32[4,8,128]{2,1,0:T(8,128)} %param.3), channel_id=1, source_target_pairs={{0,1},{1,2},{2,3},{3,4},{4,5},{5,6},{6,7},{7,8},{8,9},{9,10},{10,1... | collective-permute-start | bytes 49160 | tf_op jit(solution)/shard_map/ppermute | solution.py:140
  5.2 6.5 %collective-permute-start.1 = (s32[4,8,128]{2,1,0:T(8,128)}, s32[4,8,128]{2,1,0:T(8,128)S(1)}, u32[]{:S(2)}, u32[]{:S(2)}) collective-permute-start(s32[4,8,128]{2,1,0:T(8,128)} %param.3), channel_id=1, source_target_pairs={{1,0},{2,1},{3,2},{4,3},{5,4},{6,5},{7,6},{8,7},{9,8},{10,9},{11,1... | collective-permute-start | bytes 49160 | tf_op jit(solution)/shard_map/ppermute | solution.py:140
  10.7 1.0 %copy-start.2 = (s32[4,8,128]{2,1,0:T(8,128)S(1)}, s32[4,8,128]{2,1,0:T(8,128)}, u32[]{:S(2)}) copy-start(s32[4,8,128]{2,1,0:T(8,128)} %param.3) | copy-start | bytes 49156
  11.8 5.4 %collective-permute-start.3 = (s32[4,16,128]{2,1,0:T(8,128)S(1)}, s32[4,16,128]{2,1,0:T(8,128)S(1)}, u32[]{:S(2)}, u32[]{:S(2)}) collective-permute-start(s32[4,16,128]{2,1,0:T(8,128)S(1)} %pad_add_fusion.mid_ref), channel_id=1, source_target_pairs={{32,0},{64,32},{96,64},{128,96},{160,128},{192,160},{224,192},{256... | collective-permute-start | bytes 98312 | tf_op jit(solution)/shard_map/ppermute | solution.py:140
  13.1 5.0 %collective-permute-start.2 = (s32[4,16,128]{2,1,0:T(8,128)S(1)}, s32[4,16,128]{2,1,0:T(8,128)S(1)}, u32[]{:S(2)}, u32[]{:S(2)}) collective-permute-start(s32[4,16,128]{2,1,0:T(8,128)S(1)} %pad_add_fusion.mid_ref), channel_id=1, source_target_pairs={{0,32},{32,64},{64,96},{96,128},{128,160},{160,192},{192,224},{224... | collective-permute-start | bytes 98312 | tf_op jit(solution)/shard_map/ppermute | solution.py:140
  17.1 0.9 %copy-start = (s32[128]{0:T(128)S(1)}, s32[128]{0:T(128)}, u32[]{:S(2)}) copy-start(s32[128]{0:T(128)} %param.4) | copy-start | bytes 1540
  17.1 0.9 %copy-start.1 = (f32[8]{0:T(128)S(1)}, f32[8]{0:T(128)}, u32[]{:S(2)}) copy-start(f32[8]{0:T(128)} %eps_ref.3) | copy-start | bytes 100

commit v2 on v0

v2 whole, which is shorter than its diff:
```python
import jax
import jax.numpy as jnp
from jax import lax
from jax.experimental import pallas as pl
from jax.experimental.pallas import tpu as pltpu
from jax.sharding import PartitionSpec as P

K = 16
STEPS = 3
DEPTH = STEPS + 1
ROWS = 8
LANES = 128
F32, BF16 = jnp.float32, jnp.bfloat16


def split(value):
    high = value.astype(BF16)
    rest = value - high.astype(F32)
    middle = rest.astype(BF16)
    return high, middle, (rest - middle.astype(F32)).astype(BF16)


def basis_kernel(low_ref, mid_ref, high_ref, coef_ref, split_ref, moments_ref, weight, b0, b1, b2, b3):
    nx, wide, nz = mid_ref.shape
    ny = wide - 2 * DEPTH

    def beyond(x, y):
        return max(nx - x, 0, x - 2 * nx + 1) + max(DEPTH - y, 0, y - DEPTH - ny + 1)

    shape = (K, nz)
    lateral_c, below_c, above_c, root = (jnp.broadcast_to(coef_ref[i : i + 1, :], shape) for i in range(4))
    number = lax.broadcasted_iota(jnp.int32, shape, 0) + 1
    for x in range(3 * nx):
        ref = (low_ref, mid_ref, high_ref)[x // nx]
        for y in range(wide):
            if beyond(x, y) <= DEPTH:
                label = jnp.broadcast_to(ref[x % nx, y : y + 1, :], shape)
                b0[x, y] = (label == number).astype(F32)
                if beyond(x, y) < DEPTH:
                    weight[x, y] = jnp.where(label == 0, lateral_c, 0.0)[:ROWS]
    powers = (b0, b1, b2, b3)
    for level in range(1, DEPTH + 1):
        source = powers[level - 1]
        for x in range(3 * nx):
            for y in range(wide):
                if beyond(x, y) > DEPTH - level:
                    continue
                centre = source[x, y]
                lateral = (source[x - 1, y] + source[x + 1, y]) + (source[x, y - 1] + source[x, y + 1])
                vertical = below_c * pltpu.roll(centre, 1, 1) + above_c * pltpu.roll(centre, nz - 1, 1)
                factor = weight[x, y]
                value = jnp.concatenate([factor, factor], 0) * (lateral + vertical)
                if level < DEPTH:
                    powers[level][x, y] = value
                if beyond(x, y) == 0:
                    cell = (x - nx) * ny + y - DEPTH
                    for part, piece in enumerate(split(value * root)):
                        first = (part * DEPTH + level - 1) * K
                        split_ref[first : first + K, cell * nz : (cell + 1) * nz] = piece
    size, used = DEPTH * K, STEPS * K
    grams = lax.dot_general(
        jnp.concatenate([split_ref[part * size : part * size + used, :] for part in range(3)], 0),
        split_ref[...],
        (((1,), (1,)), ((), ())),
        preferred_element_type=F32,
    )

    def piece(i, j):
        return grams[i * used : (i + 1) * used, j * size : (j + 1) * size]

    gram = piece(0, 0) + ((piece(0, 1) + piece(1, 0)) + ((piece(0, 2) + piece(2, 0)) + piece(1, 1)))
    gram = jnp.concatenate([gram, jnp.zeros((used, LANES - size), F32)], 1)
    lane = lax.broadcasted_iota(jnp.int32, (K, LANES), 1)
    row = lax.broadcasted_iota(jnp.int32, (K, LANES), 0)
    packed = jnp.zeros((K, LANES), F32)
    for pair in range(3):
        start = pair * (K + 1)
        left, right = (pair + 3) // 2, pair // 2
        lower = pltpu.roll(gram[left * K : (left + 1) * K], (start - (pair + 4) // 2 * K) % LANES, 1)
        upper = pltpu.roll(gram[right * K : (right + 1) * K], (start + 1 - (pair + 1) // 2 * K) % LANES, 1)
        inside = (lane >= start) & (lane < start + K + 1)
        packed = jnp.where(inside, jnp.where(lane - start <= row, lower, upper), packed)
    folded = packed[:ROWS] + pltpu.roll(packed[ROWS:], LANES // 2, 1)
    for copy in range(moments_ref.shape[0]):
        moments_ref[copy] = folded


def eliminate(matrix):
    tiles = len(matrix)
    sub = lax.broadcasted_iota(jnp.int32, (ROWS, LANES), 0)
    for block in range(tiles):
        columns = [
            [
                jnp.broadcast_to(tile[:, block * ROWS + j : block * ROWS + j + 1], (ROWS, LANES))
                for tile in matrix
            ]
            for j in range(ROWS)
        ]
        for j in range(ROWS):
            column = columns[j]
            inverse = 1.0 / column[block][j : j + 1]
            line = matrix[block][j : j + 1] * inverse
            for later in range(j + 1, ROWS):
                other = columns[later]
                share = other[block][j : j + 1] * inverse
                columns[later] = [
                    jnp.where(sub == j, share, other[t] - column[t] * share) if t == block else other[t] - column[t] * share
                    for t in range(tiles)
                ]
            matrix = [
                jnp.where(sub == j, line, matrix[t] - column[t] * line) if t == block else matrix[t] - column[t] * line
                for t in range(tiles)
            ]
    return matrix


def outputs_kernel(parts_ref, split_ref, coef_ref, solution_ref, residual_ref, turned):
    ny, nz = solution_ref.shape[2:]
    cells = solution_ref.shape[1] * ny
    sums = [parts_ref[part] for part in range(parts_ref.shape[0])]
    while len(sums) > 1:
        sums = [a + b for a, b in zip(sums[::2], sums[1::2])]
    folded = sums[0]
    packed = jnp.concatenate([folded, pltpu.roll(folded, LANES // 2, 1)], 0)
    turned[...] = packed.T
    lane = lax.broadcasted_iota(jnp.int32, (K, LANES), 1)
    row = lax.broadcasted_iota(jnp.int32, (K, LANES), 0)
    moments = jnp.zeros((K, LANES), F32)
    for power in range(2 * STEPS):
        pair, upper = power % 3, power < 3
        start = pair * (K + 1) + upper
        mirrored = jnp.concatenate([turned[start : start + K, :], jnp.zeros((K, LANES - K), F32)], 1)
        direct = pltpu.roll(packed, (power * K - start) % LANES, 1)
        mirrored = pltpu.roll(mirrored, power * K, 1) if power else mirrored
        column = lane - power * K
        chosen = jnp.where(column >= row, direct, mirrored) if upper else jnp.where(column <= row, direct, mirrored)
        moments = jnp.where((column >= 0) & (column < K), chosen, moments)
    images = moments - pltpu.roll(moments, LANES - K, 1)
    matrix = []
    for power in range(STEPS):
        left = images if power == 0 else pltpu.roll(images, LANES - power * K, 1)
        right = pltpu.roll(moments, (STEPS - power) * K, 1)
        block = jnp.where(lane < STEPS * K, left, right)
        matrix += [block[:ROWS], block[ROWS:]]
    matrix = jnp.concatenate(eliminate(matrix), 0)
    weights = matrix[:, STEPS * K : (STEPS + 1) * K].T
    first, second, third = weights[:, :K], weights[:, K : 2 * K], weights[:, 2 * K :]
    unit = (
        lax.broadcasted_iota(jnp.int32, (K, K), 0) == lax.broadcasted_iota(jnp.int32, (K, K), 1)
    ).astype(F32)
    none = jnp.zeros((K, K), F32)
    combine = jnp.concatenate(
        [
            jnp.concatenate([first, second, third, none], 1),
            jnp.concatenate([unit - first, first - second, second - third, third], 1),
        ],
        0,
    )
    high, middle, low = split(combine)
    zero = jnp.zeros(high.shape, BF16)
    factors = jnp.concatenate(
        [
            jnp.concatenate([high, high, high], 1),
            jnp.concatenate([middle, middle, zero], 1),
            jnp.concatenate([low, zero, zero], 1),
        ],
        0,
    )
    both = jnp.dot(factors, split_ref[...], preferred_element_type=F32)
    count = 2 * K
    both = both[:count] + (both[count : 2 * count] + both[2 * count :])
    root, over = coef_ref[3:4, :], coef_ref[4:5, :]
    for cell in range(cells):
        block = both[:, cell * nz : (cell + 1) * nz]
        solution_ref[:, cell // ny, cell % ny, :] = block[:K] * over
        residual_ref[:, cell // ny, cell % ny, :] = block[K:] * root


def coefficients(layer_index, layer_eps):
    layers = jnp.arange(layer_eps.shape[0], dtype=jnp.int32)
    eps = jnp.where(layer_index[None, :] == layers[:, None], layer_eps[:, None], 0.0).sum(0)
    middle = 0.5 * (eps[1:] + eps[:-1])
    nothing = jnp.zeros((1,), F32)
    down = jnp.concatenate([eps[:1], middle])
    up = jnp.concatenate([middle, eps[-1:]])
    diag = 4.0 * eps + down + up
    below = jnp.concatenate([nothing, middle]) / eps
    above = jnp.concatenate([middle, nothing]) / eps
    root = jnp.sqrt(diag)
    blank = jnp.zeros_like(eps)
    return jnp.stack([eps / diag, below, above, root, 1.0 / root, blank, blank, blank])


def neighbours(block, axis):
    count, at = lax.axis_size(axis), lax.axis_index(axis)
    even = lax.ppermute(block, axis, [(i, i ^ 1) for i in range(count)])
    pairs = [(i, i + 1) for i in range(1, count - 1, 2)]
    odd = lax.ppermute(block, axis, pairs + [(j, i) for i, j in pairs])
    second = at % 2 == 1
    before = jnp.where(second, even, jnp.where(at > 0, odd, -1))
    after = jnp.where(second, jnp.where(at < count - 1, odd, -1), even)
    return before, after


def gathered(copies, axis):
    return lax.all_to_all(copies, axis, 0, 0, tiled=True)


def on_device(labels, layer_index, layer_eps):
    nx, ny, nz = labels.shape
    wide, rows = ny + 2 * DEPTH, 3 * nx
    before, after = neighbours(labels, "gy")
    mid = jnp.concatenate([before[:, ny - DEPTH :], labels, after[:, :DEPTH]], 1)
    low, high = neighbours(mid, "gx")
    coef = coefficients(layer_index, layer_eps)
    vmem = pl.BlockSpec(memory_space=pltpu.VMEM)
    params = pltpu.CompilerParams(vmem_limit_bytes=16 << 20)
    in_x, in_y = lax.axis_size("gx"), lax.axis_size("gy")
    field = pltpu.VMEM((rows, wide, K, nz), F32)
    parts, moments = pl.pallas_call(
        basis_kernel,
        out_shape=(
            jax.ShapeDtypeStruct((3 * DEPTH * K, nx * ny * nz), BF16),
            jax.ShapeDtypeStruct((in_y, ROWS, LANES), F32),
        ),
        in_specs=[vmem] * 4,
        out_specs=(vmem, vmem),
        scratch_shapes=[pltpu.VMEM((rows, wide, ROWS, nz), F32), field, field, field, field],
        compiler_params=params,
    )(low, mid, high, coef)
    total = gathered(moments, "gy").sum(0)
    sums = gathered(jnp.broadcast_to(total[None], (in_x,) + total.shape), "gx")
    block = jax.ShapeDtypeStruct((K, nx, ny, nz), F32)
    return pl.pallas_call(
        outputs_kernel,
        out_shape=(block, block),
        in_specs=[vmem] * 3,
        out_specs=(vmem, vmem),
        scratch_shapes=[pltpu.VMEM((LANES, K), F32)],
        compiler_params=params,
    )(sums, parts, coef)


def solution(mesh):
    return jax.shard_map(
        on_device,
        mesh=mesh,
        in_specs=(P("gx", "gy", None), P(), P()),
        out_specs=(P(None, "gx", "gy", None), P(None, "gx", "gy", None)),
        check_vma=False,
    )
```

time: 971 us -> 65.5 us (0.07)
  blocking collectives: 818 us -> 39.1 us
  matrix products: 66.8 us -> 0 us
  starting transfers between devices: 45.5 us -> 13.3 us
  waiting for transfers between devices: 17.5 us -> 3.2 us
    psum x8 -> x0, blocking collectives: 818 us -> none  [the longest x3 322 us: on_device(): curvature = lax.psum(local_gram(search, image), ('gx', 'gy'))]
    dot_general x71 -> x0, matrix products: 66.8 us -> none  [the longest x48 55.8 us: lower_inverse(): jnp.dot(factor[row], inverse, precision=lax.Precision.HIGHEST)]
    all_to_all x0 -> x2, blocking collectives: none -> 39.1 us  [gathered(): return lax.all_to_all(copies, axis, 0, 0, tiled=True)]
    ppermute x16 -> x4, starting transfers between devices: 45.5 us -> 13.3 us  [the longest x2 10.7 us: neighbours(): even = lax.ppermute(block, axis, [(i, i ^ 1) for i in range(count)])]
    ppermute x16 -> x4, waiting for transfers between devices: 17.5 us -> 3.2 us  [the longest x2 2.64 us: neighbours(): even = lax.ppermute(block, axis, [(i, i ^ 1) for i in range(count)])]
  transfers between devices with their start and end apart: 16 -> 4, of which waited for: 8 -> 2; matrix products, arithmetic and copies ran while one was open for 0% -> 4% of each run, Pallas kernels for 0% -> 0%
where the time goes in v2:
time: 65.5 us; the launch traced here: 65.1 us
  blocking collectives  39.1 us (60%)
  starting transfers between devices  13.3 us (20%)
  Pallas kernels  5.17 us (8%)
  waiting for transfers between devices  3.2 us (5%)
  other arithmetic  2.99 us (5%)
  between operations  0.73 us (1%)
    all_to_all x2, blocking collectives, gathered(): return lax.all_to_all(copies, axis, 0, 0, tiled=True)  39.1 us
    ppermute x2, starting transfers between devices, neighbours(): even = lax.ppermute(block, axis, [(i, i ^ 1) for i in range(count)])  10.7 us
    pallas_call x1, Pallas kernels, on_device(): pl.pallas_call(outputs_kernel, out_shape=(block, block), in_specs=[vmem]...  3.16 us
    ppermute x2, waiting for transfers between devices, neighbours(): even = lax.ppermute(block, axis, [(i, i ^ 1) for i in range(count)])  2.64 us
    ppermute x2, starting transfers between devices, neighbours(): odd = lax.ppermute(block, axis, pairs + [(j, i) for i, j in pairs])  2.58 us
    pallas_call x1, Pallas kernels, on_device(): pl.pallas_call(basis_kernel, out_shape=(jax.ShapeDtypeStruct((3 * DEPTH *...  2.01 us
    div x1, other arithmetic, coefficients(): above = jnp.concatenate([middle, nothing]) / eps  1.37 us
  transfers between devices with their start and end apart: 4, of which 2 were waited for; matrix products, arithmetic and copies ran while one was open for 4% of the time, Pallas kernels for 0%

profile of v2, /device:TPU:1, one launch (start us, length us, event | category | flops | bytes accessed | tf_op | source)
XLA Modules:
  0.0 65.1 jit_solution(10405880418181363246)
XLA Ops:
  0.6 8.8 %collective-permute-start = (s32[4,8,128]{2,1,0:T(8,128)}, s32[4,8,128]{2,1,0:T(8,128)S(1)}, u32[]{:S(2)}, u32[]{:S(2)}) collective-permute-start(s32[4,8,128]{2,1,0:T(8,128)} %param.3), channel_id=1, source_target_pairs={{0,1},{1,0},{2,3},{3,2},{4,5},{5,4},{6,7},{7,6},{8,9},{9,8},{10,11... | collective-permute-start | bytes 49160 | tf_op jit(solution)/shard_map/ppermute | solution.py:196
  9.4 1.9 %collective-permute-start.1 = (s32[4,8,128]{2,1,0:T(8,128)}, s32[4,8,128]{2,1,0:T(8,128)S(1)}, u32[]{:S(2)}, u32[]{:S(2)}) collective-permute-start(s32[4,8,128]{2,1,0:T(8,128)} %param.3), channel_id=1, source_target_pairs={{1,2},{3,4},{5,6},{7,8},{9,10},{11,12},{13,14},{15,16},{17,18},{19... | collective-permute-start | bytes 49160 | tf_op jit(solution)/shard_map/ppermute | solution.py:198
  11.4 0.8 %select_reduce_fusion = f32[128]{0:T(128)S(1)} fusion(f32[8]{0:T(128)} %param.5, s32[128]{0:T(128)} %param.4), kind=kLoop, calls=%fused_computation.7 | loop fusion | flops 2944 | bytes 1056 | tf_op jit(solution)/shard_map/reduce_sum | solution.py:181
  12.1 0.1 multiply_bitcast_fusion
  12.2 0.6 fusion.4
  12.8 1.4 %maximum_divide_fusion.1 = (f32[1,128]{1,0:T(1,128)S(1)}, f32[1,128]{1,0:T(1,128)S(1)}, f32[1,128]{1,0:T(1,128)S(1)}, f32[1,128]{1,0:T(1,128)S(1)}) fusion(f32[1,1]{1,0:T(1,128)} %constant.46.clone.1, f32[128]{0:T(128)S(1)} %select_reduce_fusion, f32[1,127]{1,0:T(1,128)S(1)} %multiply_bitcast_fusion, f32[1,1]{1,0:T(1,128)} %bitcast.3, f32[1,1]{1,0:T(1,128)} %bitcast.1), kind=kLoop, calls=%fused_computation.12 | loop fusion | flops 1152 | bytes 3080 | tf_op jit(solution)/shard_map/div | solution.py:188
  14.1 0.0 collective-permute-done
  14.1 0.6 collective-permute-done.1
  14.7 0.7 %pad_add_fusion.mid_ref = s32[4,16,128]{2,1,0:T(8,128)S(1)} fusion(s32[4,4,128]{2,1,0:T(4,128)S(1)} %get-tuple-element.11, s32[4,8,128]{2,1,0:T(8,128)} %param.3, s32[4,4,128]{2,1,0:T(4,128)S(1)} %get-tuple-element.10), kind=kLoop, calls=%fused_computation | loop fusion | flops 16384 | bytes 65536 | tf_op jit(solution)/shard_map/concatenate | solution.py:213
  15.4 0.7 %collective-permute-start.3 = (s32[4,16,128]{2,1,0:T(8,128)S(1)}, s32[4,16,128]{2,1,0:T(8,128)S(1)}, u32[]{:S(2)}, u32[]{:S(2)}) collective-permute-start(s32[4,16,128]{2,1,0:T(8,128)S(1)} %pad_add_fusion.mid_ref), channel_id=1, source_target_pairs={{32,64},{96,128},{160,192},{224,256},{288,320},{352,384},{416,448}... | collective-permute-start | bytes 98312 | tf_op jit(solution)/shard_map/ppermute | solution.py:198
  16.1 1.9 %collective-permute-start.2 = (s32[4,16,128]{2,1,0:T(8,128)S(1)}, s32[4,16,128]{2,1,0:T(8,128)S(1)}, u32[]{:S(2)}, u32[]{:S(2)}) collective-permute-start(s32[4,16,128]{2,1,0:T(8,128)S(1)} %pad_add_fusion.mid_ref), channel_id=1, source_target_pairs={{0,32},{32,0},{64,96},{96,64},{128,160},{160,128},{192,224},{224,1... | collective-permute-start | bytes 98312 | tf_op jit(solution)/shard_map/ppermute | solution.py:196
  18.1 0.0 collective-permute-done.3
  18.1 2.6 %collective-permute-done.2 = s32[4,16,128]{2,1,0:T(8,128)S(1)} collective-permute-done((s32[4,16,128]{2,1,0:T(8,128)S(1)}, s32[4,16,128]{2,1,0:T(8,128)S(1)}, u32[]{:S(2)}, u32[]{:S(2)}) %collective-permute-start.2) | collective-permute-done | bytes 32800 | tf_op jit(solution)/shard_map/ppermute | solution.py:196
  20.8 2.0 %shard_map.50 = (bf16[192,4096]{1,0:T(8,128)(2,1)S(1)}, f32[32,8,128]{2,1,0:T(8,128)S(1)}) custom-call(s32[4,16,128]{2,1,0:T(8,128)S(1)} %get-tuple-element.9.low_ref, s32[4,16,128]{2,1,0:T(8,128)S(1)} %pad_add_fusion.mid_ref, s32[4,16,128]{2,1,0:T(8,128)S(1)} %get-tuple-element.8.high_ref, f32[8,128]{1,0:T(8,128)S(1)} %stack.5.coef_ref), custom_call_target="tpu_custom_call" | custom-call | tf_op jit(solution)/shard_map/pallas_call | solution.py:220
  22.8 14.3 %all_to_all.10 = f32[32,8,128]{2,1,0:T(8,128)S(1)} all-to-all(f32[32,8,128]{2,1,0:T(8,128)S(1)} %get-tuple-element.4), channel_id=1, replica_groups=mesh['gx'=16,'gy'=32] {'gy'}, dimensions={0} | all-to-all | bytes 262144 | tf_op jit(solution)/shard_map/all_to_all | solution.py:206
  37.2 24.8 %all_to_all.11.parts_ref = f32[16,8,128]{2,1,0:T(8,128)S(1)} all-to-all(f32[16,8,128]{2,1,0:T(8,128)S(1)} %broadcast_in_dim.35), channel_id=1, replica_groups=mesh['gx'=16,'gy'=32] {'gx'}, dimensions={0} | all-to-all | bytes 131072 | tf_op jit(solution)/shard_map/all_to_all | solution.py:206
  61.9 3.2 %shard_map.51 = (f32[16,4,8,128]{3,2,1,0:T(8,128)}, f32[16,4,8,128]{3,2,1,0:T(8,128)}) custom-call(f32[16,8,128]{2,1,0:T(8,128)S(1)} %all_to_all.11.parts_ref, bf16[192,4096]{1,0:T(8,128)(2,1)S(1)} %get-tuple-element.5.split_ref, f32[8,128]{1,0:T(8,128)S(1)} %stack.5.coef_ref), custom_call_target="tpu_custom_call" | custom-call | tf_op jit(solution)/shard_map/pallas_call | solution.py:234
  (8 shorter events, 0.1 us)
Async XLA Ops:
  0.6 13.5 %collective-permute-start = (s32[4,8,128]{2,1,0:T(8,128)}, s32[4,8,128]{2,1,0:T(8,128)S(1)}, u32[]{:S(2)}, u32[]{:S(2)}) collective-permute-start(s32[4,8,128]{2,1,0:T(8,128)} %param.3), channel_id=1, source_target_pairs={{0,1},{1,0},{2,3},{3,2},{4,5},{5,4},{6,7},{7,6},{8,9},{9,8},{10,11... | collective-permute-start | bytes 49160 | tf_op jit(solution)/shard_map/ppermute | solution.py:196
  9.4 5.3 %collective-permute-start.1 = (s32[4,8,128]{2,1,0:T(8,128)}, s32[4,8,128]{2,1,0:T(8,128)S(1)}, u32[]{:S(2)}, u32[]{:S(2)}) collective-permute-start(s32[4,8,128]{2,1,0:T(8,128)} %param.3), channel_id=1, source_target_pairs={{1,2},{3,4},{5,6},{7,8},{9,10},{11,12},{13,14},{15,16},{17,18},{19... | collective-permute-start | bytes 49160 | tf_op jit(solution)/shard_map/ppermute | solution.py:198
  15.4 2.7 %collective-permute-start.3 = (s32[4,16,128]{2,1,0:T(8,128)S(1)}, s32[4,16,128]{2,1,0:T(8,128)S(1)}, u32[]{:S(2)}, u32[]{:S(2)}) collective-permute-start(s32[4,16,128]{2,1,0:T(8,128)S(1)} %pad_add_fusion.mid_ref), channel_id=1, source_target_pairs={{32,64},{96,128},{160,192},{224,256},{288,320},{352,384},{416,448}... | collective-permute-start | bytes 98312 | tf_op jit(solution)/shard_map/ppermute | solution.py:198
  16.1 4.7 %collective-permute-start.2 = (s32[4,16,128]{2,1,0:T(8,128)S(1)}, s32[4,16,128]{2,1,0:T(8,128)S(1)}, u32[]{:S(2)}, u32[]{:S(2)}) collective-permute-start(s32[4,16,128]{2,1,0:T(8,128)S(1)} %pad_add_fusion.mid_ref), channel_id=1, source_target_pairs={{0,32},{32,0},{64,96},{96,64},{128,160},{160,128},{192,224},{224,1... | collective-permute-start | bytes 98312 | tf_op jit(solution)/shard_map/ppermute | solution.py:196

commit v3 on v2

--- a/solution.py
+++ b/solution.py
@@ -176,19 +176,27 @@
         residual_ref[:, cell // ny, cell % ny, :] = block[K:] * root
 
 
-def coefficients(layer_index, layer_eps):
-    layers = jnp.arange(layer_eps.shape[0], dtype=jnp.int32)
-    eps = jnp.where(layer_index[None, :] == layers[:, None], layer_eps[:, None], 0.0).sum(0)
-    middle = 0.5 * (eps[1:] + eps[:-1])
-    nothing = jnp.zeros((1,), F32)
-    down = jnp.concatenate([eps[:1], middle])
-    up = jnp.concatenate([middle, eps[-1:]])
+def plane_kernel(index_ref, eps_ref, late_ref, coef_ref):
+    del late_ref
+    index = index_ref[...]
+    eps = jnp.zeros(index.shape, F32)
+    for layer in range(eps_ref.shape[1]):
+        eps = jnp.where(index == layer, jnp.broadcast_to(eps_ref[:, layer : layer + 1], index.shape), eps)
+    count = index.shape[1]
+    lane = lax.broadcasted_iota(jnp.int32, index.shape, 1)
+    down = jnp.where(lane == 0, eps, 0.5 * (eps + pltpu.roll(eps, 1, 1)))
+    up = jnp.where(lane == count - 1, eps, 0.5 * (eps + pltpu.roll(eps, count - 1, 1)))
     diag = 4.0 * eps + down + up
-    below = jnp.concatenate([nothing, middle]) / eps
-    above = jnp.concatenate([middle, nothing]) / eps
     root = jnp.sqrt(diag)
-    blank = jnp.zeros_like(eps)
-    return jnp.stack([eps / diag, below, above, root, 1.0 / root, blank, blank, blank])
+    coef_ref[0:1, :] = eps / diag
+    coef_ref[1:2, :] = jnp.where(lane == 0, 0.0, down / eps)
+    coef_ref[2:3, :] = jnp.where(lane == count - 1, 0.0, up / eps)
+    coef_ref[3:4, :] = root
+    coef_ref[4:5, :] = 1.0 / root
+
+
+def hold_kernel(given_ref, held_ref):
+    held_ref[...] = given_ref[...]
 
 
 def neighbours(block, axis):
@@ -196,9 +204,13 @@
     even = lax.ppermute(block, axis, [(i, i ^ 1) for i in range(count)])
     pairs = [(i, i + 1) for i in range(1, count - 1, 2)]
     odd = lax.ppermute(block, axis, pairs + [(j, i) for i, j in pairs])
-    second = at % 2 == 1
-    before = jnp.where(second, even, jnp.where(at > 0, odd, -1))
-    after = jnp.where(second, jnp.where(at < count - 1, odd, -1), even)
+    first = at % 2 == 0
+    if axis == "gy":
+        before = jnp.where(first, jnp.where(at > 0, odd, -1), even)
+        after = jnp.where(first, even, jnp.where(at < count - 1, odd, -1))
+    else:
+        before = jnp.where(~first, even, jnp.where(at > 0, odd, -1))
+        after = jnp.where(~first, jnp.where(at < count - 1, odd, -1), even)
     return before, after
 
 
@@ -209,12 +221,25 @@
 def on_device(labels, layer_index, layer_eps):
     nx, ny, nz = labels.shape
     wide, rows = ny + 2 * DEPTH, 3 * nx
-    before, after = neighbours(labels, "gy")
-    mid = jnp.concatenate([before[:, ny - DEPTH :], labels, after[:, :DEPTH]], 1)
-    low, high = neighbours(mid, "gx")
-    coef = coefficients(layer_index, layer_eps)
     vmem = pl.BlockSpec(memory_space=pltpu.VMEM)
     params = pltpu.CompilerParams(vmem_limit_bytes=16 << 20)
+    held = pl.pallas_call(
+        hold_kernel,
+        out_shape=jax.ShapeDtypeStruct(labels.shape, labels.dtype),
+        in_specs=[vmem],
+        out_specs=vmem,
+        compiler_params=params,
+    )(labels)
+    before, after = neighbours(labels, "gy")
+    mid = jnp.concatenate([before[:, ny - DEPTH :], held, after[:, :DEPTH]], 1)
+    low, high = neighbours(mid, "gx")
+    coef = pl.pallas_call(
+        plane_kernel,
+        out_shape=jax.ShapeDtypeStruct((ROWS, nz), F32),
+        in_specs=[vmem, vmem, pl.BlockSpec(memory_space=pl.ANY)],
+        out_specs=vmem,
+        compiler_params=params,
+    )(layer_index.reshape(1, nz), layer_eps.reshape(1, -1), mid)
     in_x, in_y = lax.axis_size("gx"), lax.axis_size("gy")
     field = pltpu.VMEM((rows, wide, K, nz), F32)
     parts, moments = pl.pallas_call(

time: 65.5 us -> 63.2 us (0.965)
  other arithmetic: 2.99 us -> 0.07 us
  waiting for transfers between devices: 3.2 us -> 0.3 us
  local copies, waits for them, and re-layouts: 0.62 us -> 2.02 us
  blocking collectives: 39.1 us -> 40.4 us
    ppermute x2, starting transfers between devices: 2.58 us -> 5.26 us  [neighbours(): odd = lax.ppermute(block, axis, pairs + [(j, i) for i, j in pairs])]
    ppermute x2, waiting for transfers between devices: 2.64 us -> 0.29 us  [neighbours(): even = lax.ppermute(block, axis, [(i, i ^ 1) for i in range(count)])]
    ppermute x2, starting transfers between devices: 10.7 us -> 8.68 us  [neighbours(): even = lax.ppermute(block, axis, [(i, i ^ 1) for i in range(count)])]
    unnamed x0 -> x6, local copies, waits for them, and re-layouts: none -> 2.02 us
    div x1 -> x0, other arithmetic: 1.37 us -> none  [coefficients(): above = jnp.concatenate([middle, nothing]) / eps]
    all_to_all x2, blocking collectives: 39.1 us -> 40.4 us  [gathered(): return lax.all_to_all(copies, axis, 0, 0, tiled=True)]
    concatenate x2 -> x1, other arithmetic: 0.81 us -> 0.01 us  [on_device(): mid = jnp.concatenate([before[:, ny - DEPTH:], held, after[:, :DEPTH]], 1)]
    reduce_sum x1 -> x0, other arithmetic: 0.76 us -> none  [coefficients(): jnp.where(layer_index[None, :] == layers[:, None], layer_eps[:, None], 0.0)]
  transfers between devices with their start and end apart: 4 -> 4, of which waited for: 2 -> 1; matrix products, arithmetic and copies ran while one was open for 4% -> 0% of each run, Pallas kernels for 0% -> 0%
where the time goes in v3:
time: 63.2 us; the launch traced here: 62.9 us
  blocking collectives  40.4 us (64%)
  starting transfers between devices  13.9 us (22%)
  Pallas kernels  5.34 us (8%)
  local copies, waits for them, and re-layouts  2.02 us (3%)
  between operations  0.75 us (1%)
    all_to_all x2, blocking collectives, gathered(): return lax.all_to_all(copies, axis, 0, 0, tiled=True)  40.4 us
    ppermute x2, starting transfers between devices, neighbours(): even = lax.ppermute(block, axis, [(i, i ^ 1) for i in range(count)])  8.68 us
    ppermute x2, starting transfers between devices, neighbours(): odd = lax.ppermute(block, axis, pairs + [(j, i) for i, j in pairs])  5.26 us
    pallas_call x1, Pallas kernels, on_device(): pl.pallas_call(outputs_kernel, out_shape=(block, block), in_specs=[vmem]...  3.18 us
    unnamed x6, local copies, waits for them, and re-layouts  2.02 us
    pallas_call x1, Pallas kernels, on_device(): pl.pallas_call(basis_kernel, out_shape=(jax.ShapeDtypeStruct((3 * DEPTH *...  2.01 us
  transfers between devices with their start and end apart: 4, of which 1 were waited for; matrix products, arithmetic and copies ran while one was open for 0% of the time, Pallas kernels for 0%

profile of v3, /device:TPU:1, one launch (start us, length us, event | category | flops | bytes accessed | tf_op | source)
XLA Modules:
  0.0 62.9 jit_solution(8549022767472938684)
XLA Ops:
  0.6 4.6 %collective-permute-start = (s32[4,8,128]{2,1,0:T(8,128)}, s32[4,8,128]{2,1,0:T(8,128)S(1)}, u32[]{:S(2)}, u32[]{:S(2)}) collective-permute-start(s32[4,8,128]{2,1,0:T(8,128)} %given_ref.1), channel_id=1, source_target_pairs={{1,2},{3,4},{5,6},{7,8},{9,10},{11,12},{13,14},{15,16},{17,18},{19... | collective-permute-start | bytes 49160 | tf_op jit(solution)/shard_map/ppermute | solution.py:206
  5.2 4.9 %collective-permute-start.1 = (s32[4,8,128]{2,1,0:T(8,128)}, s32[4,8,128]{2,1,0:T(8,128)S(1)}, u32[]{:S(2)}, u32[]{:S(2)}) collective-permute-start(s32[4,8,128]{2,1,0:T(8,128)} %given_ref.1), channel_id=1, source_target_pairs={{0,1},{1,0},{2,3},{3,2},{4,5},{5,4},{6,7},{7,6},{8,9},{9,8},{10,11... | collective-permute-start | bytes 49160 | tf_op jit(solution)/shard_map/ppermute | solution.py:204
  10.1 0.0 copy-start
  10.1 0.7 %copy-done = s32[4,8,128]{2,1,0:T(8,128)S(1)} copy-done((s32[4,8,128]{2,1,0:T(8,128)S(1)}, s32[4,8,128]{2,1,0:T(8,128)}, u32[]{:S(2)}) %copy-start) | copy-done | bytes 16408
  10.8 0.0 collective-permute-done
  10.8 0.3 collective-permute-done.1
  11.2 0.7 %collective-permute-start.3 = (s32[4,16,128]{2,1,0:T(8,128)S(1)}, s32[4,16,128]{2,1,0:T(8,128)S(1)}, u32[]{:S(2)}, u32[]{:S(2)}) collective-permute-start(s32[4,16,128]{2,1,0:T(8,128)S(1)} %pad_add_fusion.late_ref.mid_ref), channel_id=1, source_target_pairs={{32,64},{96,128},{160,192},{224,256},{288,320},{352,384},{416,448}... | collective-permute-start | bytes 98312 | tf_op jit(solution)/shard_map/ppermute | solution.py:206
  11.8 3.8 %collective-permute-start.2 = (s32[4,16,128]{2,1,0:T(8,128)S(1)}, s32[4,16,128]{2,1,0:T(8,128)S(1)}, u32[]{:S(2)}, u32[]{:S(2)}) collective-permute-start(s32[4,16,128]{2,1,0:T(8,128)S(1)} %pad_add_fusion.late_ref.mid_ref), channel_id=1, source_target_pairs={{0,32},{32,0},{64,96},{96,64},{128,160},{160,128},{192,224},{224,1... | collective-permute-start | bytes 98312 | tf_op jit(solution)/shard_map/ppermute | solution.py:204
  15.7 0.0 copy-start.1
  15.7 0.6 %copy-done.1 = s32[128]{0:T(128)S(1)} copy-done((s32[128]{0:T(128)S(1)}, s32[128]{0:T(128)}, u32[]{:S(2)}) %copy-start.1) | copy-done | bytes 536
  16.3 0.0 copy-start.2
  16.3 0.7 %copy-done.2 = f32[8]{0:T(128)S(1)} copy-done((f32[8]{0:T(128)S(1)}, f32[8]{0:T(128)}, u32[]{:S(2)}) %copy-start.2) | copy-done | bytes 56
  17.0 0.1 shard_map.51.coef_ref
  17.1 0.0 collective-permute-done.3
  17.2 0.0 collective-permute-done.2
  17.2 2.0 %shard_map.52 = (bf16[192,4096]{1,0:T(8,128)(2,1)S(1)}, f32[32,8,128]{2,1,0:T(8,128)S(1)}) custom-call(s32[4,16,128]{2,1,0:T(8,128)S(1)} %get-tuple-element.7.low_ref, s32[4,16,128]{2,1,0:T(8,128)S(1)} %pad_add_fusion.late_ref.mid_ref, s32[4,16,128]{2,1,0:T(8,128)S(1)} %get-tuple-element.6.high_ref, f32[8,128]{1,0:T(8,128)S(1)} %shard_map.51.coef_ref), custom_call_target="tpu_custom_call" | custom-call | tf_op jit(solution)/shard_map/pallas_call | solution.py:245
  19.2 15.4 %all_to_all.10 = f32[32,8,128]{2,1,0:T(8,128)S(1)} all-to-all(f32[32,8,128]{2,1,0:T(8,128)S(1)} %get-tuple-element.4), channel_id=1, replica_groups=mesh['gx'=16,'gy'=32] {'gy'}, dimensions={0} | all-to-all | bytes 262144 | tf_op jit(solution)/shard_map/all_to_all | solution.py:218
  34.6 25.1 %all_to_all.11.parts_ref = f32[16,8,128]{2,1,0:T(8,128)S(1)} all-to-all(f32[16,8,128]{2,1,0:T(8,128)S(1)} %broadcast_in_dim.18), channel_id=1, replica_groups=mesh['gx'=16,'gy'=32] {'gx'}, dimensions={0} | all-to-all | bytes 131072 | tf_op jit(solution)/shard_map/all_to_all | solution.py:218
  59.7 3.2 %shard_map.53 = (f32[16,4,8,128]{3,2,1,0:T(8,128)}, f32[16,4,8,128]{3,2,1,0:T(8,128)}) custom-call(f32[16,8,128]{2,1,0:T(8,128)S(1)} %all_to_all.11.parts_ref, bf16[192,4096]{1,0:T(8,128)(2,1)S(1)} %get-tuple-element.5.split_ref, f32[8,128]{1,0:T(8,128)S(1)} %shard_map.51.coef_ref), custom_call_target="tpu_custom_call" | custom-call | tf_op jit(solution)/shard_map/pallas_call | solution.py:259
  (6 shorter events, 0.1 us)
Async XLA Ops:
  0.6 10.2 %collective-permute-start = (s32[4,8,128]{2,1,0:T(8,128)}, s32[4,8,128]{2,1,0:T(8,128)S(1)}, u32[]{:S(2)}, u32[]{:S(2)}) collective-permute-start(s32[4,8,128]{2,1,0:T(8,128)} %given_ref.1), channel_id=1, source_target_pairs={{1,2},{3,4},{5,6},{7,8},{9,10},{11,12},{13,14},{15,16},{17,18},{19... | collective-permute-start | bytes 49160 | tf_op jit(solution)/shard_map/ppermute | solution.py:206
  5.2 5.9 %collective-permute-start.1 = (s32[4,8,128]{2,1,0:T(8,128)}, s32[4,8,128]{2,1,0:T(8,128)S(1)}, u32[]{:S(2)}, u32[]{:S(2)}) collective-permute-start(s32[4,8,128]{2,1,0:T(8,128)} %given_ref.1), channel_id=1, source_target_pairs={{0,1},{1,0},{2,3},{3,2},{4,5},{5,4},{6,7},{7,6},{8,9},{9,8},{10,11... | collective-permute-start | bytes 49160 | tf_op jit(solution)/shard_map/ppermute | solution.py:204
  10.1 0.7 %copy-start = (s32[4,8,128]{2,1,0:T(8,128)S(1)}, s32[4,8,128]{2,1,0:T(8,128)}, u32[]{:S(2)}) copy-start(s32[4,8,128]{2,1,0:T(8,128)} %given_ref.1) | copy-start | bytes 49156
  11.2 6.0 %collective-permute-start.3 = (s32[4,16,128]{2,1,0:T(8,128)S(1)}, s32[4,16,128]{2,1,0:T(8,128)S(1)}, u32[]{:S(2)}, u32[]{:S(2)}) collective-permute-start(s32[4,16,128]{2,1,0:T(8,128)S(1)} %pad_add_fusion.late_ref.mid_ref), channel_id=1, source_target_pairs={{32,64},{96,128},{160,192},{224,256},{288,320},{352,384},{416,448}... | collective-permute-start | bytes 98312 | tf_op jit(solution)/shard_map/ppermute | solution.py:206
  11.8 5.3 %collective-permute-start.2 = (s32[4,16,128]{2,1,0:T(8,128)S(1)}, s32[4,16,128]{2,1,0:T(8,128)S(1)}, u32[]{:S(2)}, u32[]{:S(2)}) collective-permute-start(s32[4,16,128]{2,1,0:T(8,128)S(1)} %pad_add_fusion.late_ref.mid_ref), channel_id=1, source_target_pairs={{0,32},{32,0},{64,96},{96,64},{128,160},{160,128},{192,224},{224,1... | collective-permute-start | bytes 98312 | tf_op jit(solution)/shard_map/ppermute | solution.py:204
  15.7 0.7 %copy-start.1 = (s32[128]{0:T(128)S(1)}, s32[128]{0:T(128)}, u32[]{:S(2)}) copy-start(s32[128]{0:T(128)} %param.4) | copy-start | bytes 1540
  16.3 0.7 %copy-start.2 = (f32[8]{0:T(128)S(1)}, f32[8]{0:T(128)}, u32[]{:S(2)}) copy-start(f32[8]{0:T(128)} %param.5) | copy-start | bytes 100

commit v4 on v3

--- a/solution.py
+++ b/solution.py
@@ -20,39 +20,75 @@
     return high, middle, (rest - middle.astype(F32)).astype(BF16)
 
 
-def basis_kernel(low_ref, mid_ref, high_ref, coef_ref, split_ref, moments_ref, weight, b0, b1, b2, b3):
-    nx, wide, nz = mid_ref.shape
-    ny = wide - 2 * DEPTH
-
-    def beyond(x, y):
-        return max(nx - x, 0, x - 2 * nx + 1) + max(DEPTH - y, 0, y - DEPTH - ny + 1)
-
-    shape = (K, nz)
-    lateral_c, below_c, above_c, root = (jnp.broadcast_to(coef_ref[i : i + 1, :], shape) for i in range(4))
-    number = lax.broadcasted_iota(jnp.int32, shape, 0) + 1
-    for x in range(3 * nx):
-        ref = (low_ref, mid_ref, high_ref)[x // nx]
+def beyond(x, y, nx, ny):
+    return max(nx - x, 0, x - 2 * nx + 1) + max(DEPTH - y, 0, y - DEPTH - ny + 1)
+
+
+def is_early(level, x, y, nx, ny):
+    return DEPTH + level <= y < DEPTH + ny - level and level <= x < 3 * nx - level
+
+
+def excite(label, lateral_c):
+    label = jnp.broadcast_to(label, lateral_c.shape)
+    number = lax.broadcasted_iota(jnp.int32, lateral_c.shape, 0) + 1
+    return (label == number).astype(F32), jnp.where(label == 0, lateral_c, 0.0)[:ROWS]
+
+
+def next_power(x, y, power, factor, below_c, above_c):
+    centre = power(x, y)
+    lateral = (power(x - 1, y) + power(x + 1, y)) + (power(x, y - 1) + power(x, y + 1))
+    last = centre.shape[1] - 1
+    vertical = below_c * pltpu.roll(centre, 1, 1) + above_c * pltpu.roll(centre, last, 1)
+    return jnp.concatenate([factor, factor], 0) * (lateral + vertical)
+
+
+def early_kernel(centre_ref, coef_ref, weight, b0, b1, b2, b3):
+    rows, ny, nz = centre_ref.shape
+    nx = rows // 3
+    lateral_c, below_c, above_c = (jnp.broadcast_to(coef_ref[i : i + 1, :], (K, nz)) for i in range(3))
+    for x in range(rows):
+        for y in range(ny):
+            b0[x, y], weight[x, y] = excite(centre_ref[x, y : y + 1, :], lateral_c)
+    powers = (b0, b1, b2, b3)
+    for level in range(1, DEPTH):
+        source = powers[level - 1]
+        for x in range(rows):
+            for y in range(ny):
+                if is_early(level, x, y + DEPTH, nx, ny):
+                    powers[level][x, y] = next_power(
+                        x, y, lambda i, j, source=source: source[i, j], weight[x, y], below_c, above_c
+                    )
+
+
+def basis_kernel(left_ref, right_ref, coef_ref, early_weight, e0, e1, e2, e3, split_ref, moments_ref, weight, b0, b1, b2, b3):
+    rows, ny, _, nz = early_weight.shape
+    nx, wide = rows // 3, ny + 2 * DEPTH
+    lateral_c, below_c, above_c, root = (jnp.broadcast_to(coef_ref[i : i + 1, :], (K, nz)) for i in range(4))
+    for x in range(rows):
         for y in range(wide):
-            if beyond(x, y) <= DEPTH:
-                label = jnp.broadcast_to(ref[x % nx, y : y + 1, :], shape)
-                b0[x, y] = (label == number).astype(F32)
-                if beyond(x, y) < DEPTH:
-                    weight[x, y] = jnp.where(label == 0, lateral_c, 0.0)[:ROWS]
-    powers = (b0, b1, b2, b3)
+            if beyond(x, y, nx, ny) <= DEPTH and not is_early(0, x, y, nx, ny):
+                ref, at = (left_ref, y) if y < DEPTH else (right_ref, y - DEPTH - ny)
+                b0[x, y], weight[x, y] = excite(ref[x, at : at + 1, :], lateral_c)
+    early, late = (e0, e1, e2, e3), (b0, b1, b2, b3)
+
+    def power(level, x, y):
+        return early[level][x, y - DEPTH] if is_early(level, x, y, nx, ny) else late[level][x, y]
+
     for level in range(1, DEPTH + 1):
-        source = powers[level - 1]
-        for x in range(3 * nx):
+        for x in range(rows):
             for y in range(wide):
-                if beyond(x, y) > DEPTH - level:
+                if beyond(x, y, nx, ny) > DEPTH - level:
                     continue
-                centre = source[x, y]
-                lateral = (source[x - 1, y] + source[x + 1, y]) + (source[x, y - 1] + source[x, y + 1])
-                vertical = below_c * pltpu.roll(centre, 1, 1) + above_c * pltpu.roll(centre, nz - 1, 1)
-                factor = weight[x, y]
-                value = jnp.concatenate([factor, factor], 0) * (lateral + vertical)
-                if level < DEPTH:
-                    powers[level][x, y] = value
-                if beyond(x, y) == 0:
+                if is_early(level, x, y, nx, ny):
+                    value = power(level, x, y)
+                else:
+                    factor = early_weight[x, y - DEPTH] if is_early(0, x, y, nx, ny) else weight[x, y]
+                    value = next_power(
+                        x, y, lambda i, j, level=level: power(level - 1, i, j), factor, below_c, above_c
+                    )
+                    if level < DEPTH:
+                        late[level][x, y] = value
+                if beyond(x, y, nx, ny) == 0:
                     cell = (x - nx) * ny + y - DEPTH
                     for part, piece in enumerate(split(value * root)):
                         first = (part * DEPTH + level - 1) * K
@@ -176,8 +212,8 @@
         residual_ref[:, cell // ny, cell % ny, :] = block[K:] * root
 
 
-def plane_kernel(index_ref, eps_ref, late_ref, coef_ref):
-    del late_ref
+def plane_kernel(labels_ref, index_ref, eps_ref, held_ref, coef_ref):
+    held_ref[...] = labels_ref[...]
     index = index_ref[...]
     eps = jnp.zeros(index.shape, F32)
     for layer in range(eps_ref.shape[1]):
@@ -195,22 +231,14 @@
     coef_ref[4:5, :] = 1.0 / root
 
 
-def hold_kernel(given_ref, held_ref):
-    held_ref[...] = given_ref[...]
-
-
-def neighbours(block, axis):
+def neighbours(to_even, to_odd, axis):
     count, at = lax.axis_size(axis), lax.axis_index(axis)
-    even = lax.ppermute(block, axis, [(i, i ^ 1) for i in range(count)])
     pairs = [(i, i + 1) for i in range(1, count - 1, 2)]
-    odd = lax.ppermute(block, axis, pairs + [(j, i) for i, j in pairs])
+    odd = lax.ppermute(to_odd, axis, pairs + [(j, i) for i, j in pairs])
+    even = lax.ppermute(to_even, axis, [(i, i ^ 1) for i in range(count)])
     first = at % 2 == 0
-    if axis == "gy":
-        before = jnp.where(first, jnp.where(at > 0, odd, -1), even)
-        after = jnp.where(first, even, jnp.where(at < count - 1, odd, -1))
-    else:
-        before = jnp.where(~first, even, jnp.where(at > 0, odd, -1))
-        after = jnp.where(~first, jnp.where(at < count - 1, odd, -1), even)
+    before = jnp.where(first, jnp.where(at > 0, odd, -1), even)
+    after = jnp.where(first, even, jnp.where(at < count - 1, odd, -1))
     return before, after
 
 
@@ -223,24 +251,27 @@
     wide, rows = ny + 2 * DEPTH, 3 * nx
     vmem = pl.BlockSpec(memory_space=pltpu.VMEM)
     params = pltpu.CompilerParams(vmem_limit_bytes=16 << 20)
-    held = pl.pallas_call(
-        hold_kernel,
-        out_shape=jax.ShapeDtypeStruct(labels.shape, labels.dtype),
-        in_specs=[vmem],
-        out_specs=vmem,
+    held, coef = pl.pallas_call(
+        plane_kernel,
+        out_shape=(jax.ShapeDtypeStruct(labels.shape, labels.dtype), jax.ShapeDtypeStruct((ROWS, nz), F32)),
+        in_specs=[vmem] * 3,
+        out_specs=(vmem, vmem),
         compiler_params=params,
-    )(labels)
-    before, after = neighbours(labels, "gy")
-    mid = jnp.concatenate([before[:, ny - DEPTH :], held, after[:, :DEPTH]], 1)
-    low, high = neighbours(mid, "gx")
-    coef = pl.pallas_call(
-        plane_kernel,
-        out_shape=jax.ShapeDtypeStruct((ROWS, nz), F32),
-        in_specs=[vmem, vmem, pl.BlockSpec(memory_space=pl.ANY)],
-        out_specs=vmem,
+    )(labels, layer_index.reshape(1, nz), layer_eps.reshape(1, -1))
+    low, high = neighbours(labels, labels, "gx")
+    centre = jnp.concatenate([low, held, high], 0)
+    first, last = centre[:, :DEPTH], centre[:, ny - DEPTH :]
+    second = lax.axis_index("gy") % 2 == 1
+    left, right = neighbours(jnp.where(second, first, last), jnp.where(second, last, first), "gy")
+    in_x, in_y = lax.axis_size("gx"), lax.axis_size("gy")
+    early = pl.pallas_call(
+        early_kernel,
+        out_shape=[jax.ShapeDtypeStruct((rows, ny, ROWS, nz), F32)]
+        + [jax.ShapeDtypeStruct((rows, ny, K, nz), F32)] * DEPTH,
+        in_specs=[vmem] * 2,
+        out_specs=[vmem] * (1 + DEPTH),
         compiler_params=params,
-    )(layer_index.reshape(1, nz), layer_eps.reshape(1, -1), mid)
-    in_x, in_y = lax.axis_size("gx"), lax.axis_size("gy")
+    )(centre, coef)
     field = pltpu.VMEM((rows, wide, K, nz), F32)
     parts, moments = pl.pallas_call(
         basis_kernel,
@@ -248,11 +279,11 @@
             jax.ShapeDtypeStruct((3 * DEPTH * K, nx * ny * nz), BF16),
             jax.ShapeDtypeStruct((in_y, ROWS, LANES), F32),
         ),
-        in_specs=[vmem] * 4,
+        in_specs=[vmem] * (4 + DEPTH),
         out_specs=(vmem, vmem),
-        scratch_shapes=[pltpu.VMEM((rows, wide, ROWS, nz), F32), field, field, field, field],
+        scratch_shapes=[pltpu.VMEM((rows, wide, ROWS, nz), F32)] + [field] * DEPTH,
         compiler_params=params,
-    )(low, mid, high, coef)
+    )(left, right, coef, *early)
     total = gathered(moments, "gy").sum(0)
     sums = gathered(jnp.broadcast_to(total[None], (in_x,) + total.shape), "gx")
     block = jax.ShapeDtypeStruct((K, nx, ny, nz), F32)

time: 63.2 us -> 62.9 us (level)
  blocking collectives: 40.4 us -> 39.2 us
    all_to_all x2, blocking collectives: 40.4 us -> 39.2 us  [gathered(): return lax.all_to_all(copies, axis, 0, 0, tiled=True)]
  transfers between devices with their start and end apart: 4 -> 4, of which waited for: 1 -> 1; matrix products, arithmetic and copies ran while one was open for 0% -> 0% of each run, Pallas kernels for 0% -> 1%
where the time goes in v4:
time: 62.9 us; the launch traced here: 62.5 us
  blocking collectives  39.2 us (62%)
  starting transfers between devices  14.2 us (23%)
  Pallas kernels  5.54 us (9%)
  local copies, waits for them, and re-layouts  2.05 us (3%)
  between operations  0.77 us (1%)
  waiting for transfers between devices  0.72 us (1%)
    all_to_all x2, blocking collectives, gathered(): return lax.all_to_all(copies, axis, 0, 0, tiled=True)  39.2 us
    ppermute x2, starting transfers between devices, neighbours(): even = lax.ppermute(to_even, axis, [(i, i ^ 1) for i in range(count)])  9.18 us
    ppermute x2, starting transfers between devices, neighbours(): odd = lax.ppermute(to_odd, axis, pairs + [(j, i) for i, j in pairs])  4.99 us
    pallas_call x1, Pallas kernels, on_device(): pl.pallas_call(outputs_kernel, out_shape=(block, block), in_specs=[vmem]...  3.18 us
    unnamed x6, local copies, waits for them, and re-layouts  2.04 us
    pallas_call x1, Pallas kernels, on_device(): pl.pallas_call(basis_kernel, out_shape=(jax.ShapeDtypeStruct((3 * DEPTH *...  1.78 us
  transfers between devices with their start and end apart: 4, of which 1 were waited for; matrix products, arithmetic and copies ran while one was open for 0% of the time, Pallas kernels for 1%

profile of v4, /device:TPU:1, one launch (start us, length us, event | category | flops | bytes accessed | tf_op | source)
XLA Modules:
  0.0 62.5 jit_solution(8785827443021331584)
XLA Ops:
  0.6 0.7 %collective-permute-start = (s32[4,8,128]{2,1,0:T(8,128)}, s32[4,8,128]{2,1,0:T(8,128)S(1)}, u32[]{:S(2)}, u32[]{:S(2)}) collective-permute-start(s32[4,8,128]{2,1,0:T(8,128)} %labels_ref.1), channel_id=1, source_target_pairs={{32,64},{96,128},{160,192},{224,256},{288,320},{352,384},{416,448}... | collective-permute-start | bytes 49160 | tf_op jit(solution)/shard_map/ppermute | solution.py:237
  1.3 7.3 %collective-permute-start.1 = (s32[4,8,128]{2,1,0:T(8,128)}, s32[4,8,128]{2,1,0:T(8,128)S(1)}, u32[]{:S(2)}, u32[]{:S(2)}) collective-permute-start(s32[4,8,128]{2,1,0:T(8,128)} %labels_ref.1), channel_id=1, source_target_pairs={{0,32},{32,0},{64,96},{96,64},{128,160},{160,128},{192,224},{224,1... | collective-permute-start | bytes 49160 | tf_op jit(solution)/shard_map/ppermute | solution.py:238
  8.6 0.0 copy-start
  8.6 0.7 %copy-done = s32[4,8,128]{2,1,0:T(8,128)S(1)} copy-done((s32[4,8,128]{2,1,0:T(8,128)S(1)}, s32[4,8,128]{2,1,0:T(8,128)}, u32[]{:S(2)}) %copy-start) | copy-done | bytes 16408
  9.3 0.0 copy-start.1
  9.3 0.7 %copy-done.1 = s32[128]{0:T(128)S(1)} copy-done((s32[128]{0:T(128)S(1)}, s32[128]{0:T(128)}, u32[]{:S(2)}) %copy-start.1) | copy-done | bytes 536
  10.0 0.0 copy-start.2
  10.0 0.7 %copy-done.2 = f32[8]{0:T(128)S(1)} copy-done((f32[8]{0:T(128)S(1)}, f32[8]{0:T(128)}, u32[]{:S(2)}) %copy-start.2) | copy-done | bytes 56
  10.6 0.1 shard_map.50
  10.8 0.0 collective-permute-done
  10.8 0.0 collective-permute-done.1
  10.9 4.3 %collective-permute-start.2 = (s32[12,4,128]{2,1,0:T(4,128)S(1)}, s32[12,4,128]{2,1,0:T(4,128)S(1)}, u32[]{:S(2)}, u32[]{:S(2)}) collective-permute-start(s32[12,4,128]{2,1,0:T(4,128)S(1)} %get-tuple-element.22), channel_id=1, source_target_pairs={{1,2},{3,4},{5,6},{7,8},{9,10},{11,12},{13,14},{15,16},{17,18},{19... | collective-permute-start | bytes 73736 | tf_op jit(solution)/shard_map/ppermute | solution.py:237
  15.2 1.9 %collective-permute-start.3 = (s32[12,4,128]{2,1,0:T(4,128)S(1)}, s32[12,4,128]{2,1,0:T(4,128)S(1)}, u32[]{:S(2)}, u32[]{:S(2)}) collective-permute-start(s32[12,4,128]{2,1,0:T(4,128)S(1)} %get-tuple-element.23), channel_id=1, source_target_pairs={{0,1},{1,0},{2,3},{3,2},{4,5},{5,4},{6,7},{7,6},{8,9},{9,8},{10,11... | collective-permute-start | bytes 73736 | tf_op jit(solution)/shard_map/ppermute | solution.py:238
  17.1 0.4 shard_map.51
  17.6 0.0 collective-permute-done.2
  17.6 0.7 %collective-permute-done.3 = s32[12,4,128]{2,1,0:T(4,128)S(1)} collective-permute-done((s32[12,4,128]{2,1,0:T(4,128)S(1)}, s32[12,4,128]{2,1,0:T(4,128)S(1)}, u32[]{:S(2)}, u32[]{:S(2)}) %collective-permute-start.3) | collective-permute-done | bytes 24608 | tf_op jit(solution)/shard_map/ppermute | solution.py:238
  18.3 1.8 %shard_map.52 = (bf16[192,4096]{1,0:T(8,128)(2,1)S(1)}, f32[32,8,128]{2,1,0:T(8,128)S(1)}) custom-call(s32[12,4,128]{2,1,0:T(4,128)S(1)} %get-tuple-element.21.left_ref, s32[12,4,128]{2,1,0:T(4,128)S(1)} %get-tuple-element.20.right_ref, f32[8,128]{1,0:T(8,128)S(1)} %get-tuple-element.12.coef_ref, f32[12,8,8,128]{3,2,1,0:T(8,128)S(1)} %get-tuple-element.13.early_weight, ...), custom_call_target="tpu_custom_call" | custom-call | tf_op jit(solution)/shard_map/pallas_call | solution.py:276
  20.1 14.5 %all_to_all.10 = f32[32,8,128]{2,1,0:T(8,128)S(1)} all-to-all(f32[32,8,128]{2,1,0:T(8,128)S(1)} %get-tuple-element.18), channel_id=1, replica_groups=mesh['gx'=16,'gy'=32] {'gy'}, dimensions={0} | all-to-all | bytes 262144 | tf_op jit(solution)/shard_map/all_to_all | solution.py:246
  34.6 24.7 %all_to_all.11.parts_ref = f32[16,8,128]{2,1,0:T(8,128)S(1)} all-to-all(f32[16,8,128]{2,1,0:T(8,128)S(1)} %broadcast_in_dim.18), channel_id=1, replica_groups=mesh['gx'=16,'gy'=32] {'gx'}, dimensions={0} | all-to-all | bytes 131072 | tf_op jit(solution)/shard_map/all_to_all | solution.py:246
  59.3 3.2 %shard_map.53 = (f32[16,4,8,128]{3,2,1,0:T(8,128)}, f32[16,4,8,128]{3,2,1,0:T(8,128)}) custom-call(f32[16,8,128]{2,1,0:T(8,128)S(1)} %all_to_all.11.parts_ref, bf16[192,4096]{1,0:T(8,128)(2,1)S(1)} %get-tuple-element.19.split_ref, f32[8,128]{1,0:T(8,128)S(1)} %get-tuple-element.12.coef_ref), custom_call_target="tpu_custom_call" | custom-call | tf_op jit(solution)/shard_map/pallas_call | solution.py:290
  (6 shorter events, 0.1 us)
Async XLA Ops:
  0.6 10.2 %collective-permute-start = (s32[4,8,128]{2,1,0:T(8,128)}, s32[4,8,128]{2,1,0:T(8,128)S(1)}, u32[]{:S(2)}, u32[]{:S(2)}) collective-permute-start(s32[4,8,128]{2,1,0:T(8,128)} %labels_ref.1), channel_id=1, source_target_pairs={{32,64},{96,128},{160,192},{224,256},{288,320},{352,384},{416,448}... | collective-permute-start | bytes 49160 | tf_op jit(solution)/shard_map/ppermute | solution.py:237
  1.3 9.5 %collective-permute-start.1 = (s32[4,8,128]{2,1,0:T(8,128)}, s32[4,8,128]{2,1,0:T(8,128)S(1)}, u32[]{:S(2)}, u32[]{:S(2)}) collective-permute-start(s32[4,8,128]{2,1,0:T(8,128)} %labels_ref.1), channel_id=1, source_target_pairs={{0,32},{32,0},{64,96},{96,64},{128,160},{160,128},{192,224},{224,1... | collective-permute-start | bytes 49160 | tf_op jit(solution)/shard_map/ppermute | solution.py:238
  8.6 0.7 %copy-start = (s32[4,8,128]{2,1,0:T(8,128)S(1)}, s32[4,8,128]{2,1,0:T(8,128)}, u32[]{:S(2)}) copy-start(s32[4,8,128]{2,1,0:T(8,128)} %labels_ref.1) | copy-start | bytes 49156
  9.3 0.7 %copy-start.1 = (s32[128]{0:T(128)S(1)}, s32[128]{0:T(128)}, u32[]{:S(2)}) copy-start(s32[128]{0:T(128)} %param.4) | copy-start | bytes 1540
  10.0 0.7 %copy-start.2 = (f32[8]{0:T(128)S(1)}, f32[8]{0:T(128)}, u32[]{:S(2)}) copy-start(f32[8]{0:T(128)} %param.5) | copy-start | bytes 100
  10.9 6.7 %collective-permute-start.2 = (s32[12,4,128]{2,1,0:T(4,128)S(1)}, s32[12,4,128]{2,1,0:T(4,128)S(1)}, u32[]{:S(2)}, u32[]{:S(2)}) collective-permute-start(s32[12,4,128]{2,1,0:T(4,128)S(1)} %get-tuple-element.22), channel_id=1, source_target_pairs={{1,2},{3,4},{5,6},{7,8},{9,10},{11,12},{13,14},{15,16},{17,18},{19... | collective-permute-start | bytes 73736 | tf_op jit(solution)/shard_map/ppermute | solution.py:237
  15.2 3.1 %collective-permute-start.3 = (s32[12,4,128]{2,1,0:T(4,128)S(1)}, s32[12,4,128]{2,1,0:T(4,128)S(1)}, u32[]{:S(2)}, u32[]{:S(2)}) collective-permute-start(s32[12,4,128]{2,1,0:T(4,128)S(1)} %get-tuple-element.23), channel_id=1, source_target_pairs={{0,1},{1,0},{2,3},{3,2},{4,5},{5,4},{6,7},{7,6},{8,9},{9,8},{10,11... | collective-permute-start | bytes 73736 | tf_op jit(solution)/shard_map/ppermute | solution.py:238

commit v5 on v4

--- a/solution.py
+++ b/solution.py
@@ -150,9 +150,9 @@
     return matrix
 
 
-def outputs_kernel(parts_ref, split_ref, coef_ref, solution_ref, residual_ref, turned):
+def outputs_kernel(parts_ref, split_ref, coef_ref, solution_out, residual_out, turned, solution_ref, residual_ref, sent):
     ny, nz = solution_ref.shape[2:]
-    cells = solution_ref.shape[1] * ny
+    width = ny * nz
     sums = [parts_ref[part] for part in range(parts_ref.shape[0])]
     while len(sums) > 1:
         sums = [a + b for a, b in zip(sums[::2], sums[1::2])]
@@ -202,14 +202,21 @@
         ],
         0,
     )
-    both = jnp.dot(factors, split_ref[...], preferred_element_type=F32)
     count = 2 * K
-    both = both[:count] + (both[count : 2 * count] + both[2 * count :])
     root, over = coef_ref[3:4, :], coef_ref[4:5, :]
-    for cell in range(cells):
-        block = both[:, cell * nz : (cell + 1) * nz]
-        solution_ref[:, cell // ny, cell % ny, :] = block[:K] * over
-        residual_ref[:, cell // ny, cell % ny, :] = block[K:] * root
+    copies = []
+    for x in range(solution_ref.shape[1]):
+        both = jnp.dot(factors, split_ref[:, x * width : (x + 1) * width], preferred_element_type=F32)
+        both = both[:count] + (both[count : 2 * count] + both[2 * count :])
+        for y in range(ny):
+            block = both[:, y * nz : (y + 1) * nz]
+            solution_ref[:, x, y, :] = block[:K] * over
+            residual_ref[:, x, y, :] = block[K:] * root
+        for i, (source, target) in enumerate(((solution_ref, solution_out), (residual_ref, residual_out))):
+            copies.append(pltpu.make_async_copy(source.at[:, x], target.at[:, x], sent.at[i, x]))
+            copies[-1].start()
+    for copy in copies:
+        copy.wait()
 
 
 def plane_kernel(labels_ref, index_ref, eps_ref, held_ref, coef_ref):
@@ -291,8 +298,13 @@
         outputs_kernel,
         out_shape=(block, block),
         in_specs=[vmem] * 3,
-        out_specs=(vmem, vmem),
-        scratch_shapes=[pltpu.VMEM((LANES, K), F32)],
+        out_specs=(pl.BlockSpec(memory_space=pl.ANY),) * 2,
+        scratch_shapes=[
+            pltpu.VMEM((LANES, K), F32),
+            pltpu.VMEM(block.shape, F32),
+            pltpu.VMEM(block.shape, F32),
+            pltpu.SemaphoreType.DMA((2, nx)),
+        ],
         compiler_params=params,
     )(sums, parts, coef)
 

time: 62.9 us -> 62.8 us (level)
  no operation moved by 1% of the time
where the time goes in v5:
time: 62.8 us; the launch traced here: 62.4 us
  blocking collectives  39.2 us (62%)
  starting transfers between devices  14.2 us (23%)
  Pallas kernels  5.47 us (9%)
  local copies, waits for them, and re-layouts  2.05 us (3%)
  between operations  0.77 us (1%)
  waiting for transfers between devices  0.72 us (1%)
    all_to_all x2, blocking collectives, gathered(): return lax.all_to_all(copies, axis, 0, 0, tiled=True)  39.2 us
    ppermute x2, starting transfers between devices, neighbours(): even = lax.ppermute(to_even, axis, [(i, i ^ 1) for i in range(count)])  9.18 us
    ppermute x2, starting transfers between devices, neighbours(): odd = lax.ppermute(to_odd, axis, pairs + [(j, i) for i, j in pairs])  4.99 us
    pallas_call x1, Pallas kernels, on_device(): pl.pallas_call(outputs_kernel, out_shape=(block, block), in_specs=[vmem]...  3.12 us
    unnamed x6, local copies, waits for them, and re-layouts  2.04 us
    pallas_call x1, Pallas kernels, on_device(): pl.pallas_call(basis_kernel, out_shape=(jax.ShapeDtypeStruct((3 * DEPTH *...  1.78 us
  transfers between devices with their start and end apart: 4, of which 1 were waited for; matrix products, arithmetic and copies ran while one was open for 0% of the time, Pallas kernels for 1%

profile of v5, /device:TPU:1, one launch (start us, length us, event | category | flops | bytes accessed | tf_op | source)
XLA Modules:
  0.0 62.4 jit_solution(8469722281029254259)
XLA Ops:
  0.6 0.7 %collective-permute-start = (s32[4,8,128]{2,1,0:T(8,128)}, s32[4,8,128]{2,1,0:T(8,128)S(1)}, u32[]{:S(2)}, u32[]{:S(2)}) collective-permute-start(s32[4,8,128]{2,1,0:T(8,128)} %labels_ref.1), channel_id=1, source_target_pairs={{32,64},{96,128},{160,192},{224,256},{288,320},{352,384},{416,448}... | collective-permute-start | bytes 49160 | tf_op jit(solution)/shard_map/ppermute | solution.py:244
  1.3 7.3 %collective-permute-start.1 = (s32[4,8,128]{2,1,0:T(8,128)}, s32[4,8,128]{2,1,0:T(8,128)S(1)}, u32[]{:S(2)}, u32[]{:S(2)}) collective-permute-start(s32[4,8,128]{2,1,0:T(8,128)} %labels_ref.1), channel_id=1, source_target_pairs={{0,32},{32,0},{64,96},{96,64},{128,160},{160,128},{192,224},{224,1... | collective-permute-start | bytes 49160 | tf_op jit(solution)/shard_map/ppermute | solution.py:245
  8.6 0.0 copy-start
  8.6 0.7 %copy-done = s32[4,8,128]{2,1,0:T(8,128)S(1)} copy-done((s32[4,8,128]{2,1,0:T(8,128)S(1)}, s32[4,8,128]{2,1,0:T(8,128)}, u32[]{:S(2)}) %copy-start) | copy-done | bytes 16408
  9.3 0.0 copy-start.1
  9.3 0.7 %copy-done.1 = s32[128]{0:T(128)S(1)} copy-done((s32[128]{0:T(128)S(1)}, s32[128]{0:T(128)}, u32[]{:S(2)}) %copy-start.1) | copy-done | bytes 536
  10.0 0.0 copy-start.2
  10.0 0.7 %copy-done.2 = f32[8]{0:T(128)S(1)} copy-done((f32[8]{0:T(128)S(1)}, f32[8]{0:T(128)}, u32[]{:S(2)}) %copy-start.2) | copy-done | bytes 56
  10.6 0.1 shard_map.50
  10.8 0.0 collective-permute-done
  10.8 0.0 collective-permute-done.1
  10.9 4.3 %collective-permute-start.2 = (s32[12,4,128]{2,1,0:T(4,128)S(1)}, s32[12,4,128]{2,1,0:T(4,128)S(1)}, u32[]{:S(2)}, u32[]{:S(2)}) collective-permute-start(s32[12,4,128]{2,1,0:T(4,128)S(1)} %get-tuple-element.22), channel_id=1, source_target_pairs={{1,2},{3,4},{5,6},{7,8},{9,10},{11,12},{13,14},{15,16},{17,18},{19... | collective-permute-start | bytes 73736 | tf_op jit(solution)/shard_map/ppermute | solution.py:244
  15.2 1.9 %collective-permute-start.3 = (s32[12,4,128]{2,1,0:T(4,128)S(1)}, s32[12,4,128]{2,1,0:T(4,128)S(1)}, u32[]{:S(2)}, u32[]{:S(2)}) collective-permute-start(s32[12,4,128]{2,1,0:T(4,128)S(1)} %get-tuple-element.23), channel_id=1, source_target_pairs={{0,1},{1,0},{2,3},{3,2},{4,5},{5,4},{6,7},{7,6},{8,9},{9,8},{10,11... | collective-permute-start | bytes 73736 | tf_op jit(solution)/shard_map/ppermute | solution.py:245
  17.1 0.4 shard_map.51
  17.6 0.0 collective-permute-done.2
  17.6 0.7 %collective-permute-done.3 = s32[12,4,128]{2,1,0:T(4,128)S(1)} collective-permute-done((s32[12,4,128]{2,1,0:T(4,128)S(1)}, s32[12,4,128]{2,1,0:T(4,128)S(1)}, u32[]{:S(2)}, u32[]{:S(2)}) %collective-permute-start.3) | collective-permute-done | bytes 24608 | tf_op jit(solution)/shard_map/ppermute | solution.py:245
  18.3 1.8 %shard_map.52 = (bf16[192,4096]{1,0:T(8,128)(2,1)S(1)}, f32[32,8,128]{2,1,0:T(8,128)S(1)}) custom-call(s32[12,4,128]{2,1,0:T(4,128)S(1)} %get-tuple-element.21.left_ref, s32[12,4,128]{2,1,0:T(4,128)S(1)} %get-tuple-element.20.right_ref, f32[8,128]{1,0:T(8,128)S(1)} %get-tuple-element.12.coef_ref, f32[12,8,8,128]{3,2,1,0:T(8,128)S(1)} %get-tuple-element.13.early_weight, ...), custom_call_target="tpu_custom_call" | custom-call | tf_op jit(solution)/shard_map/pallas_call | solution.py:283
  20.1 14.5 %all_to_all.10 = f32[32,8,128]{2,1,0:T(8,128)S(1)} all-to-all(f32[32,8,128]{2,1,0:T(8,128)S(1)} %get-tuple-element.18), channel_id=1, replica_groups=mesh['gx'=16,'gy'=32] {'gy'}, dimensions={0} | all-to-all | bytes 262144 | tf_op jit(solution)/shard_map/all_to_all | solution.py:253
  34.6 24.7 %all_to_all.11.parts_ref = f32[16,8,128]{2,1,0:T(8,128)S(1)} all-to-all(f32[16,8,128]{2,1,0:T(8,128)S(1)} %broadcast_in_dim.18), channel_id=1, replica_groups=mesh['gx'=16,'gy'=32] {'gx'}, dimensions={0} | all-to-all | bytes 131072 | tf_op jit(solution)/shard_map/all_to_all | solution.py:253
  59.3 3.1 %shard_map.53 = (f32[16,4,8,128]{3,2,1,0:T(8,128)}, f32[16,4,8,128]{3,2,1,0:T(8,128)}) custom-call(f32[16,8,128]{2,1,0:T(8,128)S(1)} %all_to_all.11.parts_ref, bf16[192,4096]{1,0:T(8,128)(2,1)S(1)} %get-tuple-element.19.split_ref, f32[8,128]{1,0:T(8,128)S(1)} %get-tuple-element.12.coef_ref), custom_call_target="tpu_custom_call" | custom-call | tf_op jit(solution)/shard_map/pallas_call | solution.py:297
  (6 shorter events, 0.1 us)
Async XLA Ops:
  0.6 10.2 %collective-permute-start = (s32[4,8,128]{2,1,0:T(8,128)}, s32[4,8,128]{2,1,0:T(8,128)S(1)}, u32[]{:S(2)}, u32[]{:S(2)}) collective-permute-start(s32[4,8,128]{2,1,0:T(8,128)} %labels_ref.1), channel_id=1, source_target_pairs={{32,64},{96,128},{160,192},{224,256},{288,320},{352,384},{416,448}... | collective-permute-start | bytes 49160 | tf_op jit(solution)/shard_map/ppermute | solution.py:244
  1.3 9.5 %collective-permute-start.1 = (s32[4,8,128]{2,1,0:T(8,128)}, s32[4,8,128]{2,1,0:T(8,128)S(1)}, u32[]{:S(2)}, u32[]{:S(2)}) collective-permute-start(s32[4,8,128]{2,1,0:T(8,128)} %labels_ref.1), channel_id=1, source_target_pairs={{0,32},{32,0},{64,96},{96,64},{128,160},{160,128},{192,224},{224,1... | collective-permute-start | bytes 49160 | tf_op jit(solution)/shard_map/ppermute | solution.py:245
  8.6 0.7 %copy-start = (s32[4,8,128]{2,1,0:T(8,128)S(1)}, s32[4,8,128]{2,1,0:T(8,128)}, u32[]{:S(2)}) copy-start(s32[4,8,128]{2,1,0:T(8,128)} %labels_ref.1) | copy-start | bytes 49156
  9.3 0.7 %copy-start.1 = (s32[128]{0:T(128)S(1)}, s32[128]{0:T(128)}, u32[]{:S(2)}) copy-start(s32[128]{0:T(128)} %param.4) | copy-start | bytes 1540
  10.0 0.7 %copy-start.2 = (f32[8]{0:T(128)S(1)}, f32[8]{0:T(128)}, u32[]{:S(2)}) copy-start(f32[8]{0:T(128)} %param.5) | copy-start | bytes 100
  10.9 6.7 %collective-permute-start.2 = (s32[12,4,128]{2,1,0:T(4,128)S(1)}, s32[12,4,128]{2,1,0:T(4,128)S(1)}, u32[]{:S(2)}, u32[]{:S(2)}) collective-permute-start(s32[12,4,128]{2,1,0:T(4,128)S(1)} %get-tuple-element.22), channel_id=1, source_target_pairs={{1,2},{3,4},{5,6},{7,8},{9,10},{11,12},{13,14},{15,16},{17,18},{19... | collective-permute-start | bytes 73736 | tf_op jit(solution)/shard_map/ppermute | solution.py:244
  15.2 3.1 %collective-permute-start.3 = (s32[12,4,128]{2,1,0:T(4,128)S(1)}, s32[12,4,128]{2,1,0:T(4,128)S(1)}, u32[]{:S(2)}, u32[]{:S(2)}) collective-permute-start(s32[12,4,128]{2,1,0:T(4,128)S(1)} %get-tuple-element.23), channel_id=1, source_target_pairs={{0,1},{1,0},{2,3},{3,2},{4,5},{5,4},{6,7},{7,6},{8,9},{9,8},{10,11... | collective-permute-start | bytes 73736 | tf_op jit(solution)/shard_map/ppermute | solution.py:245

commit v6 on v5

--- a/solution.py
+++ b/solution.py
@@ -124,14 +124,14 @@
 def eliminate(matrix):
     tiles = len(matrix)
     sub = lax.broadcasted_iota(jnp.int32, (ROWS, LANES), 0)
+
+    def column_of(tile, at):
+        return jnp.broadcast_to(tile[:, at : at + 1], (ROWS, LANES))
+
     for block in range(tiles):
-        columns = [
-            [
-                jnp.broadcast_to(tile[:, block * ROWS + j : block * ROWS + j + 1], (ROWS, LANES))
-                for tile in matrix
-            ]
-            for j in range(ROWS)
-        ]
+        below = range(block, tiles)
+        columns = [{t: column_of(matrix[t], block * ROWS + j) for t in below} for j in range(ROWS)]
+        matrix = list(matrix)
         for j in range(ROWS):
             column = columns[j]
             inverse = 1.0 / column[block][j : j + 1]
@@ -139,14 +139,20 @@
             for later in range(j + 1, ROWS):
                 other = columns[later]
                 share = other[block][j : j + 1] * inverse
-                columns[later] = [
-                    jnp.where(sub == j, share, other[t] - column[t] * share) if t == block else other[t] - column[t] * share
-                    for t in range(tiles)
-                ]
-            matrix = [
-                jnp.where(sub == j, line, matrix[t] - column[t] * line) if t == block else matrix[t] - column[t] * line
-                for t in range(tiles)
-            ]
+                columns[later] = {t: other[t] - column[t] * share for t in below}
+                columns[later][block] = jnp.where(sub == j, share, columns[later][block])
+            for t in below:
+                cleared = matrix[t] - column[t] * line
+                matrix[t] = jnp.where(sub == j, line, cleared) if t == block else cleared
+    for block in reversed(range(tiles - 1)):
+        terms = [
+            column_of(matrix[block], t * ROWS + j) * matrix[t][j : j + 1]
+            for t in range(block + 1, tiles)
+            for j in range(ROWS)
+        ]
+        while len(terms) > 1:
+            terms = [x + y for x, y in zip(terms[::2], terms[1::2])] + ([terms[-1]] if len(terms) % 2 else [])
+        matrix[block] = matrix[block] - terms[0]
     return matrix
 
 

time: 62.8 us -> 62.7 us (level)
  no operation moved by 1% of the time
where the time goes in v6:
time: 62.7 us; the launch traced here: 62.3 us
  blocking collectives  39.2 us (63%)
  starting transfers between devices  14.2 us (23%)
  Pallas kernels  5.36 us (9%)
  local copies, waits for them, and re-layouts  2.05 us (3%)
  between operations  0.77 us (1%)
  waiting for transfers between devices  0.72 us (1%)
    all_to_all x2, blocking collectives, gathered(): return lax.all_to_all(copies, axis, 0, 0, tiled=True)  39.2 us
    ppermute x2, starting transfers between devices, neighbours(): even = lax.ppermute(to_even, axis, [(i, i ^ 1) for i in range(count)])  9.18 us
    ppermute x2, starting transfers between devices, neighbours(): odd = lax.ppermute(to_odd, axis, pairs + [(j, i) for i, j in pairs])  4.99 us
    pallas_call x1, Pallas kernels, on_device(): pl.pallas_call(outputs_kernel, out_shape=(block, block), in_specs=[vmem]...  3.01 us
    unnamed x6, local copies, waits for them, and re-layouts  2.04 us
    pallas_call x1, Pallas kernels, on_device(): pl.pallas_call(basis_kernel, out_shape=(jax.ShapeDtypeStruct((3 * DEPTH *...  1.78 us
  transfers between devices with their start and end apart: 4, of which 1 were waited for; matrix products, arithmetic and copies ran while one was open for 0% of the time, Pallas kernels for 1%

profile of v6, /device:TPU:1, one launch (start us, length us, event | category | flops | bytes accessed | tf_op | source)
XLA Modules:
  0.0 62.3 jit_solution(7246516466514103949)
XLA Ops:
  0.6 0.7 %collective-permute-start = (s32[4,8,128]{2,1,0:T(8,128)}, s32[4,8,128]{2,1,0:T(8,128)S(1)}, u32[]{:S(2)}, u32[]{:S(2)}) collective-permute-start(s32[4,8,128]{2,1,0:T(8,128)} %labels_ref.1), channel_id=1, source_target_pairs={{32,64},{96,128},{160,192},{224,256},{288,320},{352,384},{416,448}... | collective-permute-start | bytes 49160 | tf_op jit(solution)/shard_map/ppermute | solution.py:250
  1.3 7.3 %collective-permute-start.1 = (s32[4,8,128]{2,1,0:T(8,128)}, s32[4,8,128]{2,1,0:T(8,128)S(1)}, u32[]{:S(2)}, u32[]{:S(2)}) collective-permute-start(s32[4,8,128]{2,1,0:T(8,128)} %labels_ref.1), channel_id=1, source_target_pairs={{0,32},{32,0},{64,96},{96,64},{128,160},{160,128},{192,224},{224,1... | collective-permute-start | bytes 49160 | tf_op jit(solution)/shard_map/ppermute | solution.py:251
  8.6 0.0 copy-start
  8.6 0.7 %copy-done = s32[4,8,128]{2,1,0:T(8,128)S(1)} copy-done((s32[4,8,128]{2,1,0:T(8,128)S(1)}, s32[4,8,128]{2,1,0:T(8,128)}, u32[]{:S(2)}) %copy-start) | copy-done | bytes 16408
  9.3 0.0 copy-start.1
  9.3 0.7 %copy-done.1 = s32[128]{0:T(128)S(1)} copy-done((s32[128]{0:T(128)S(1)}, s32[128]{0:T(128)}, u32[]{:S(2)}) %copy-start.1) | copy-done | bytes 536
  10.0 0.0 copy-start.2
  10.0 0.7 %copy-done.2 = f32[8]{0:T(128)S(1)} copy-done((f32[8]{0:T(128)S(1)}, f32[8]{0:T(128)}, u32[]{:S(2)}) %copy-start.2) | copy-done | bytes 56
  10.6 0.1 shard_map.50
  10.8 0.0 collective-permute-done
  10.8 0.0 collective-permute-done.1
  10.9 4.3 %collective-permute-start.2 = (s32[12,4,128]{2,1,0:T(4,128)S(1)}, s32[12,4,128]{2,1,0:T(4,128)S(1)}, u32[]{:S(2)}, u32[]{:S(2)}) collective-permute-start(s32[12,4,128]{2,1,0:T(4,128)S(1)} %get-tuple-element.22), channel_id=1, source_target_pairs={{1,2},{3,4},{5,6},{7,8},{9,10},{11,12},{13,14},{15,16},{17,18},{19... | collective-permute-start | bytes 73736 | tf_op jit(solution)/shard_map/ppermute | solution.py:250
  15.2 1.9 %collective-permute-start.3 = (s32[12,4,128]{2,1,0:T(4,128)S(1)}, s32[12,4,128]{2,1,0:T(4,128)S(1)}, u32[]{:S(2)}, u32[]{:S(2)}) collective-permute-start(s32[12,4,128]{2,1,0:T(4,128)S(1)} %get-tuple-element.23), channel_id=1, source_target_pairs={{0,1},{1,0},{2,3},{3,2},{4,5},{5,4},{6,7},{7,6},{8,9},{9,8},{10,11... | collective-permute-start | bytes 73736 | tf_op jit(solution)/shard_map/ppermute | solution.py:251
  17.1 0.4 shard_map.51
  17.6 0.0 collective-permute-done.2
  17.6 0.7 %collective-permute-done.3 = s32[12,4,128]{2,1,0:T(4,128)S(1)} collective-permute-done((s32[12,4,128]{2,1,0:T(4,128)S(1)}, s32[12,4,128]{2,1,0:T(4,128)S(1)}, u32[]{:S(2)}, u32[]{:S(2)}) %collective-permute-start.3) | collective-permute-done | bytes 24608 | tf_op jit(solution)/shard_map/ppermute | solution.py:251
  18.3 1.8 %shard_map.52 = (bf16[192,4096]{1,0:T(8,128)(2,1)S(1)}, f32[32,8,128]{2,1,0:T(8,128)S(1)}) custom-call(s32[12,4,128]{2,1,0:T(4,128)S(1)} %get-tuple-element.21.left_ref, s32[12,4,128]{2,1,0:T(4,128)S(1)} %get-tuple-element.20.right_ref, f32[8,128]{1,0:T(8,128)S(1)} %get-tuple-element.12.coef_ref, f32[12,8,8,128]{3,2,1,0:T(8,128)S(1)} %get-tuple-element.13.early_weight, ...), custom_call_target="tpu_custom_call" | custom-call | tf_op jit(solution)/shard_map/pallas_call | solution.py:289
  20.1 14.5 %all_to_all.10 = f32[32,8,128]{2,1,0:T(8,128)S(1)} all-to-all(f32[32,8,128]{2,1,0:T(8,128)S(1)} %get-tuple-element.18), channel_id=1, replica_groups=mesh['gx'=16,'gy'=32] {'gy'}, dimensions={0} | all-to-all | bytes 262144 | tf_op jit(solution)/shard_map/all_to_all | solution.py:259
  34.6 24.7 %all_to_all.11.parts_ref = f32[16,8,128]{2,1,0:T(8,128)S(1)} all-to-all(f32[16,8,128]{2,1,0:T(8,128)S(1)} %broadcast_in_dim.18), channel_id=1, replica_groups=mesh['gx'=16,'gy'=32] {'gx'}, dimensions={0} | all-to-all | bytes 131072 | tf_op jit(solution)/shard_map/all_to_all | solution.py:259
  59.3 3.0 %shard_map.53 = (f32[16,4,8,128]{3,2,1,0:T(8,128)}, f32[16,4,8,128]{3,2,1,0:T(8,128)}) custom-call(f32[16,8,128]{2,1,0:T(8,128)S(1)} %all_to_all.11.parts_ref, bf16[192,4096]{1,0:T(8,128)(2,1)S(1)} %get-tuple-element.19.split_ref, f32[8,128]{1,0:T(8,128)S(1)} %get-tuple-element.12.coef_ref), custom_call_target="tpu_custom_call" | custom-call | tf_op jit(solution)/shard_map/pallas_call | solution.py:303
  (6 shorter events, 0.1 us)
Async XLA Ops:
  0.6 10.2 %collective-permute-start = (s32[4,8,128]{2,1,0:T(8,128)}, s32[4,8,128]{2,1,0:T(8,128)S(1)}, u32[]{:S(2)}, u32[]{:S(2)}) collective-permute-start(s32[4,8,128]{2,1,0:T(8,128)} %labels_ref.1), channel_id=1, source_target_pairs={{32,64},{96,128},{160,192},{224,256},{288,320},{352,384},{416,448}... | collective-permute-start | bytes 49160 | tf_op jit(solution)/shard_map/ppermute | solution.py:250
  1.3 9.5 %collective-permute-start.1 = (s32[4,8,128]{2,1,0:T(8,128)}, s32[4,8,128]{2,1,0:T(8,128)S(1)}, u32[]{:S(2)}, u32[]{:S(2)}) collective-permute-start(s32[4,8,128]{2,1,0:T(8,128)} %labels_ref.1), channel_id=1, source_target_pairs={{0,32},{32,0},{64,96},{96,64},{128,160},{160,128},{192,224},{224,1... | collective-permute-start | bytes 49160 | tf_op jit(solution)/shard_map/ppermute | solution.py:251
  8.6 0.7 %copy-start = (s32[4,8,128]{2,1,0:T(8,128)S(1)}, s32[4,8,128]{2,1,0:T(8,128)}, u32[]{:S(2)}) copy-start(s32[4,8,128]{2,1,0:T(8,128)} %labels_ref.1) | copy-start | bytes 49156
  9.3 0.7 %copy-start.1 = (s32[128]{0:T(128)S(1)}, s32[128]{0:T(128)}, u32[]{:S(2)}) copy-start(s32[128]{0:T(128)} %param.4) | copy-start | bytes 1540
  10.0 0.7 %copy-start.2 = (f32[8]{0:T(128)S(1)}, f32[8]{0:T(128)}, u32[]{:S(2)}) copy-start(f32[8]{0:T(128)} %param.5) | copy-start | bytes 100
  10.9 6.7 %collective-permute-start.2 = (s32[12,4,128]{2,1,0:T(4,128)S(1)}, s32[12,4,128]{2,1,0:T(4,128)S(1)}, u32[]{:S(2)}, u32[]{:S(2)}) collective-permute-start(s32[12,4,128]{2,1,0:T(4,128)S(1)} %get-tuple-element.22), channel_id=1, source_target_pairs={{1,2},{3,4},{5,6},{7,8},{9,10},{11,12},{13,14},{15,16},{17,18},{19... | collective-permute-start | bytes 73736 | tf_op jit(solution)/shard_map/ppermute | solution.py:250
  15.2 3.1 %collective-permute-start.3 = (s32[12,4,128]{2,1,0:T(4,128)S(1)}, s32[12,4,128]{2,1,0:T(4,128)S(1)}, u32[]{:S(2)}, u32[]{:S(2)}) collective-permute-start(s32[12,4,128]{2,1,0:T(4,128)S(1)} %get-tuple-element.23), channel_id=1, source_target_pairs={{0,1},{1,0},{2,3},{3,2},{4,5},{5,4},{6,7},{7,6},{8,9},{9,8},{10,11... | collective-permute-start | bytes 73736 | tf_op jit(solution)/shard_map/ppermute | solution.py:251
